TPU v7x, 256 devices: a whole 4x4x8 slice. The times are simulated.
256 devices in a mesh: freq: 64 (over y, x_hi, z), tm: 4 (over x_lo, core).
Axes of the slice: x: 4 (x_hi: 2, x_lo: 2; x = x_hi * 2 + x_lo), y: 4, z: 8, core: 2. Of those that a mesh axis runs over, the one named last changes fastest.
Arguments:
- voltages: bfloat16 [512, 2, 1024, 1024], P(None, None, 'freq', 'tm'), may hold values from -6 to 6
- pattern: int32 [4, 2], replicated, may hold values from 0 to 3, as said below
- owner_map: int32 [4], replicated, may hold values from 0 to 3, each once
- channel_mask: int32 [512], P('freq'), may hold values from 0 to 1, as said below
- running_mean: float32 [4, 128, 128], P('tm'), may hold values from 2 to 32
- running_var: float32 [4, 128, 128], P('tm'), may hold values from 16 to 256
Outputs:
- stokes: float32 [4, 512, 4, 2, 128, 128], P('tm', 'freq')
- flag_weights: float32 [4, 512, 128, 128], P('tm', 'freq')
Inputs may be any that keep to these rules, and one draw needn't show every extreme that they name: `pattern`: each row is a pair of antenna block numbers, the first not above the second; no pair appears twice; the pair (0, 3) is always among them. `channel_mask`: at least one channel is usable.
All inputs are finite; a program needn't handle non-finite values.
Results may differ from a plain program's by a relative error of at most 0.0003.
Values may be sent and summed in bfloat16 or wider, within the bound.
No kernel may reach another device: no remote copies, remote signals or barrier semaphores. Data moves between devices by JAX's collectives and lax.ppermute only.
A program may use at most 128 MiB of HBM per device.

v0:
```python
import math

import jax
import jax.numpy as jnp
from jax import lax
from jax.sharding import PartitionSpec as P

BLOCK = 128


mixing = 0.25


def lookup(source, number):
    matches = jnp.arange(source.shape[0], dtype=jnp.int32) == number
    return jnp.sum(jnp.where(matches[:, None], source, 0), axis=0)


def tile_blocks(pattern, owner_map, number):
    matches = jnp.arange(owner_map.shape[0], dtype=jnp.int32) == number
    tile_id = jnp.sum(jnp.where(matches, owner_map, 0))
    corner = lookup(pattern, tile_id)
    return (corner[0], corner[1])


def signal_block(volts_now, block_id, tile_width):
    return lax.dynamic_slice_in_dim(
        volts_now, block_id * tile_width, tile_width, volts_now.ndim - 2
    )


def correlate(row_side, col_side):
    real_part = jnp.einsum(
        "...rit,...rjt->...ij", row_side, col_side, preferred_element_type=jnp.float32
    )
    rotated = jnp.stack([row_side[..., 1, :, :], -row_side[..., 0, :, :]], axis=-3)
    imag_part = jnp.einsum(
        "...rit,...rjt->...ij", rotated, col_side, preferred_element_type=jnp.float32
    )
    return jnp.stack([real_part, imag_part], axis=-3)


def to_stokes(summed, samples):
    visible = summed * (1.0 / math.sqrt(samples))
    pol_xx = visible[..., :BLOCK, :BLOCK]
    pol_xy = visible[..., :BLOCK, BLOCK:]
    pol_yx = visible[..., BLOCK:, :BLOCK]
    pol_yy = visible[..., BLOCK:, BLOCK:]
    stokes_i = pol_xx + pol_yy
    stokes_q = pol_xx - pol_yy
    stokes_u = pol_xy + pol_yx
    cross_diff = pol_xy - pol_yx
    stokes_v = jnp.stack([cross_diff[:, :, 1], -cross_diff[:, :, 0]], axis=2)
    return jnp.stack([stokes_i, stokes_q, stokes_u, stokes_v], axis=2)


def local(voltages, pattern, owner_map, channel_mask, running_mean, running_var):
    tm_count = lax.axis_size("tm")
    turned = lax.all_to_all(voltages, "freq", split_axis=0, concat_axis=2, tiled=True)
    tile_width = 2 * BLOCK
    owned_slots = owner_map.shape[0] // tm_count
    first_row = jnp.int32(0)
    pieces = []
    for offset in range(owned_slots * lax.axis_size("tm")):
        row_block, col_block = tile_blocks(pattern, owner_map, first_row + offset)
        pieces.append(
            correlate(
                signal_block(turned, row_block, tile_width),
                signal_block(turned, col_block, tile_width),
            )
        )
    summed = lax.psum_scatter(jnp.stack(pieces), "tm", scatter_dimension=0, tiled=True)
    stokes = to_stokes(summed, turned.shape[3] * tm_count)
    intensity = stokes[:, :, 0, 0] ** 2 + stokes[:, :, 0, 1] ** 2
    live_mask = channel_mask.astype(jnp.float32)[None, :, None, None]
    first_sum = jnp.sum(live_mask * intensity, axis=1)
    second_sum = jnp.sum(live_mask * intensity * intensity, axis=1)
    live_count = jnp.sum(channel_mask.astype(jnp.float32))
    first_sum, second_sum, live_count = lax.psum((first_sum, second_sum, live_count), "freq")
    first_sum = first_sum / live_count
    second_sum = second_sum / live_count
    blended_mean = (1.0 - mixing) * running_mean + mixing * first_sum
    spread = (
        (1.0 - mixing) * running_var
        + mixing * (second_sum - first_sum * first_sum)
        + mixing * (1.0 - mixing) * (first_sum - running_mean) ** 2
    )
    flag_weights = live_mask / (1.0 + (intensity - blended_mean[:, None]) ** 2 / spread[:, None])
    return (stokes, flag_weights)


def solution(mesh):
    return jax.shard_map(
        local,
        mesh=mesh,
        in_specs=(
            P(None, None, "freq", "tm"),
            P(),
            P(),
            P("freq"),
            P("tm", None, None),
            P("tm", None, None),
        ),
        out_specs=(P("tm", "freq", None, None, None, None), P("tm", "freq", None, None)),
        check_vma=False,
    )
```

profile of v0, /device:TPU:1, one launch (start us, length us, event | category | flops | bytes accessed | tf_op | source)
XLA Modules:
  0.0 1021.0 jit_solution(17822520030805913025)
XLA Ops:
  7.2 15.5 %all-to-all-start = ((bf16[512,2,16,256]{3,2,1,0:T(8,128)(2,1)}), bf16[512,2,16,256]{3,2,1,0:T(8,128)(2,1)}, u32[]{:S(2)}, u32[]{:S(2)}) async-start(bf16[512,2,16,256]{3,2,1,0:T(8,128)(2,1)} %param.6), calls=%async_computation | async-start | bytes 16777216 | tf_op jit(solution)/shard_map/all_to_all | solution.py:59
  22.7 0.0 reduce-scatter.2.cloned.1.call-start
  22.8 0.0 copy-done.6
  22.8 0.7 fusion.83
  23.5 1.2 iota_compare_fusion
  24.7 1.3 iota_compare_fusion.2
  26.0 0.2 select_reduce_fusion.3
  26.1 0.5 fusion.92
  27.3 0.6 fusion.93
  28.6 0.6 fusion.94
  29.9 0.6 fusion.95
  33.7 171.9 %all-to-all-done = bf16[512,2,16,256]{3,2,1,0:T(8,128)(2,1)} async-done(((bf16[512,2,16,256]{3,2,1,0:T(8,128)(2,1)}), bf16[512,2,16,256]{3,2,1,0:T(8,128)(2,1)}, u32[]{:S(2)}, u32[]{:S(2)}) %all-to-all-start) | async-done | bytes 8388640 | tf_op jit(solution)/shard_map/all_to_all | solution.py:59
  205.6 7.5 copy.8
  213.1 3.1 fusion.32
  216.2 1.5 copy-done
  217.7 0.7 fusion.37
  218.4 0.7 fusion.42
  219.2 3.0 constant_dynamic-slice_fusion.3
  222.2 0.7 fusion.47
  223.0 0.5 copy-done.1
  223.4 0.3 copy-done.2
  223.8 0.8 fusion.67
  224.5 0.5 maximum_bitcast_fusion
  225.0 0.8 fusion.62
  225.8 0.5 maximum_bitcast_fusion.1
  226.2 0.8 fusion.57
  227.0 0.5 maximum_bitcast_fusion.2
  227.5 0.8 fusion.52
  228.2 0.5 maximum_bitcast_fusion.3
  228.7 6.4 pad_maximum_fusion
  235.0 0.0 reduce-scatter.2.cloned.1.call-update
  235.1 0.0 all-reduce.3.cloned.1.call-start
  235.1 0.6 copy-done.7
  235.7 0.6 convert_reduce_fusion
  236.3 156.4 %psum.22 = f32[]{:T(128)} all-reduce(f32[]{:T(128)} %convert_reduce_fusion), channel_id=1, replica_groups=mesh['freq'=64,'tm'=4] {'freq'}, use_global_device_ids=true, to_apply=%region_12.13 | all-reduce | flops 1 | bytes 8 | tf_op jit(solution)/shard_map/psum | solution.py:79
  392.7 2.7 broadcast_multiply_fusion
  395.3 0.6 add_bitcast_fusion.1
  395.9 1.1 fusion.91
  396.9 0.8 multiply_reduce_fusion
  397.7 0.0 all-reduce.3.cloned.1.call-update
  397.7 1.3 maximum_bitcast_fusion.4
  399.0 0.5 pad_maximum_fusion.1
  399.5 0.0 copy-start.3
  399.5 0.0 copy-start.4
  399.5 2.3 copy.9
  401.8 609.8 %all-reduce.3.cloned.1.call-done = (f32[1,128,128]{2,1,0:T(8,128)}, f32[1,128,128]{2,1,0:T(8,128)}) async-done(((f32[1,128,128]{2,1,0:T(8,128)}, f32[1,128,128]{2,1,0:T(8,128)}), (f32[1,128,128]{2,1,0:T(8,128)}, f32[1,128,128]{2,1,0:T(8,128)})) %all-reduce.3.cloned.1.call-update) | async-done | bytes 131088 | tf_op jit(solution)/shard_map/psum | solution.py:79
  1011.7 1.5 add_bitcast_fusion.3
  1013.2 1.0 add_divide_fusion
  (11 shorter events, 0.0 us)
Async XLA Ops:
  7.2 15.6 %copy-start.6 = (s32[4]{0:T(128)S(1)}, s32[4]{0:T(128)}, u32[]{:S(2)}) copy-start(s32[4]{0:T(128)} %param.8) | copy-start | bytes 52
  7.2 18.8 %copy-start.5 = (s32[4,2]{0,1:T(2,128)S(1)}, s32[4,2]{0,1:T(2,128)}, u32[]{:S(2)}) copy-start(s32[4,2]{0,1:T(2,128)} %param.7) | copy-start | bytes 100
  7.2 198.4 %all-to-all-start = ((bf16[512,2,16,256]{3,2,1,0:T(8,128)(2,1)}), bf16[512,2,16,256]{3,2,1,0:T(8,128)(2,1)}, u32[]{:S(2)}, u32[]{:S(2)}) async-start(bf16[512,2,16,256]{3,2,1,0:T(8,128)(2,1)} %param.6), calls=%async_computation | async-start | bytes 16777216 | tf_op jit(solution)/shard_map/all_to_all | solution.py:59
  22.7 369.9 %reduce-scatter.2.cloned.1.call-start = ((), (), s32[]{:S(2)}) async-start(), calls=%async_computation.2 | async-start | bytes 20971520 | tf_op jit(solution)/shard_map/reduce_scatter | solution.py:72
  213.1 4.6 copy-start
  222.2 1.2 copy-start.1
  222.2 1.5 copy-start.2
  235.0 0.7 copy-start.7
  235.1 776.6 %all-reduce.3.cloned.1.call-start = ((), (), s32[]{:S(2)}) async-start(), calls=%async_computation.3 | async-start | bytes 262144 | tf_op jit(solution)/shard_map/psum | solution.py:79
  399.5 612.1 %copy-start.3 = (f32[1,128,128]{2,1,0:T(8,128)S(1)}, f32[1,128,128]{2,1,0:T(8,128)}, u32[]{:S(2)}) copy-start(f32[1,128,128]{2,1,0:T(8,128)} %param.10) | copy-start | bytes 196612
  399.5 612.1 %copy-start.4 = (f32[1,128,128]{2,1,0:T(8,128)S(1)}, f32[1,128,128]{2,1,0:T(8,128)}, u32[]{:S(2)}) copy-start(f32[1,128,128]{2,1,0:T(8,128)} %param.11) | copy-start | bytes 196612
Sparse Core Ops, SparseCore 0:
  235.2 151.6 reduce-scatter.1
  397.9 613.7 all-reduce.2
where the time goes:
time: 1040 us; the launch traced here: 1020 us
  waiting for transfers between devices  782 us (75%)
  blocking collectives  156 us (15%)
  other arithmetic  24.4 us (2%)
  between operations  19.4 us (2%)
  starting transfers between devices  15.6 us (2%)
  local copies, waits for them, and re-layouts  15.1 us (1%)
    psum x1, waiting for transfers between devices, local(): lax.psum((first_sum, second_sum, live_count), 'freq')  610 us
    all_to_all x1, waiting for transfers between devices, local(): lax.all_to_all(voltages, 'freq', split_axis=0, concat_axis=2, tiled=True)  172 us
    psum x1, blocking collectives, local(): lax.psum((first_sum, second_sum, live_count), 'freq')  156 us
  transfers between devices with their start and end apart: 3, of which 2 were waited for; matrix products, arithmetic and copies ran while one was open for 1% of the time, Pallas kernels for 0%

commit v1 on v0

v1 whole, which is shorter than its diff:
```python
import math

import jax
import jax.numpy as jnp
from jax import lax
from jax.experimental import pallas as pl
from jax.experimental.pallas import tpu as pltpu
from jax.sharding import PartitionSpec as P

BLOCK = 128
BOTH = ("freq", "tm")
mixing = 0.25


def nt(left, right):
    return lax.dot_general(
        left, right, (((1,), (1,)), ((), ())), preferred_element_type=jnp.float32
    )


def correlate_kernel(scale, rows_id, cols_id, live_ref, row_ref, col_ref, stokes_ref, moment_ref):
    channel = pl.program_id(1)
    pieces = row_ref.shape[2]
    width = row_ref.shape[1] * row_ref.shape[5]
    depth = row_ref.shape[6]

    def side(ref, piece, part):
        return ref[0, :, piece, 0, part].reshape(width, depth)

    real = jnp.zeros((width, width), jnp.float32)
    imag = jnp.zeros((width, width), jnp.float32)
    for piece in range(pieces):
        row_re, row_im = side(row_ref, piece, 0), side(row_ref, piece, 1)
        col_re, col_im = side(col_ref, piece, 0), side(col_ref, piece, 1)
        real += nt(row_re, col_re) + nt(row_im, col_im)
        imag += nt(row_im, col_re) - nt(row_re, col_im)
    real = real * scale
    imag = imag * scale
    low, high = slice(0, BLOCK), slice(BLOCK, 2 * BLOCK)
    i_re = real[low, low] + real[high, high]
    i_im = imag[low, low] + imag[high, high]
    stokes_ref[0, 0, 0, 0] = i_re
    stokes_ref[0, 0, 0, 1] = i_im
    stokes_ref[0, 0, 1, 0] = real[low, low] - real[high, high]
    stokes_ref[0, 0, 1, 1] = imag[low, low] - imag[high, high]
    stokes_ref[0, 0, 2, 0] = real[low, high] + real[high, low]
    stokes_ref[0, 0, 2, 1] = imag[low, high] + imag[high, low]
    stokes_ref[0, 0, 3, 0] = imag[low, high] - imag[high, low]
    stokes_ref[0, 0, 3, 1] = real[high, low] - real[low, high]
    power = i_re * i_re + i_im * i_im
    masked = power * live_ref[channel].astype(jnp.float32)

    @pl.when(channel == 0)
    def _():
        moment_ref[0, 0] = masked
        moment_ref[0, 1] = masked * power

    @pl.when(channel > 0)
    def _():
        moment_ref[0, 0] += masked
        moment_ref[0, 1] += masked * power


def correlate(turned, rows_id, cols_id, live, samples):
    blocks, per_block, pieces, channels, _, signals, depth = turned.shape
    slots = rows_id.shape[0]
    block = (1, per_block, pieces, 1, 2, signals, depth)
    return pl.pallas_call(
        lambda *refs: correlate_kernel(1.0 / math.sqrt(samples), *refs),
        grid_spec=pltpu.PrefetchScalarGridSpec(
            num_scalar_prefetch=3,
            grid=(slots, channels),
            in_specs=[
                pl.BlockSpec(block, lambda k, c, rows, cols, live: (rows[k], 0, 0, c, 0, 0, 0)),
                pl.BlockSpec(block, lambda k, c, rows, cols, live: (cols[k], 0, 0, c, 0, 0, 0)),
            ],
            out_specs=[
                pl.BlockSpec((1, 1, 4, 2, BLOCK, BLOCK), lambda k, c, *_: (k, c, 0, 0, 0, 0)),
                pl.BlockSpec((1, 2, BLOCK, BLOCK), lambda k, c, *_: (k, 0, 0, 0)),
            ],
        ),
        out_shape=[
            jax.ShapeDtypeStruct((slots, channels, 4, 2, BLOCK, BLOCK), jnp.float32),
            jax.ShapeDtypeStruct((slots, 2, BLOCK, BLOCK), jnp.float32),
        ],
        compiler_params=pltpu.CompilerParams(vmem_limit_bytes=32 << 20),
        cost_estimate=pl.CostEstimate(
            flops=slots * channels * 8 * (2 * BLOCK) ** 2 * samples,
            bytes_accessed=slots * channels * (4 << 20),
            transcendentals=0,
        ),
        name="correlate",
    )(rows_id, cols_id, live, turned, turned)


def local(voltages, pattern, owner_map, channel_mask, running_mean, running_var):
    freq_count, tm_count = lax.axis_size("freq"), lax.axis_size("tm")
    blocks = 4
    everyone = freq_count * tm_count
    total, _, signals, depth = voltages.shape
    mine = total // everyone
    ordered = pattern[owner_map]
    rows_id, cols_id = ordered[:, 0], ordered[:, 1]
    turned = lax.all_to_all(voltages, BOTH, split_axis=0, concat_axis=0, tiled=True)
    turned = turned.reshape(
        blocks, freq_count // blocks, tm_count, mine, 2, signals, depth
    )
    live = lax.dynamic_slice_in_dim(channel_mask, lax.axis_index("tm") * mine, mine, 0)
    stokes, moments = correlate(turned, rows_id, cols_id, live, depth * tm_count)
    slots = rows_id.shape[0]
    stokes = lax.all_to_all(
        stokes.reshape((slots * mine,) + stokes.shape[2:]), "tm", split_axis=0, concat_axis=0, tiled=True
    )
    stokes = stokes.reshape((1,) + stokes.shape)
    count_row = jnp.broadcast_to(
        jnp.sum(live.astype(jnp.float32)), (slots, freq_count, 1, BLOCK)
    )
    sent = moments.reshape(slots, 2, freq_count, BLOCK // freq_count, BLOCK)
    sent = sent.transpose(2, 0, 1, 3, 4).reshape(everyone, -1, BLOCK)
    rows = sent.shape[1]
    sent = jnp.concatenate([sent, count_row.reshape(everyone, 1, BLOCK)], axis=1)
    summed = jnp.sum(
        lax.all_to_all(sent, BOTH, split_axis=0, concat_axis=0, tiled=True).reshape(
            everyone, rows + 1, BLOCK
        ),
        axis=0,
    )
    planes = summed[:rows] / summed[rows:]
    planes = lax.all_to_all(
        jnp.broadcast_to(planes, (freq_count,) + planes.shape), "freq", 0, 0, tiled=True
    )
    planes = planes.reshape(freq_count, 2, BLOCK // freq_count, BLOCK).transpose(1, 0, 2, 3)
    first, second = planes.reshape(2, 1, BLOCK, BLOCK)
    intensity = stokes[:, :, 0, 0] ** 2 + stokes[:, :, 0, 1] ** 2
    live_mask = channel_mask.astype(jnp.float32)[None, :, None, None]
    blended = (1.0 - mixing) * running_mean + mixing * first
    spread = (
        (1.0 - mixing) * running_var
        + mixing * (second - first * first)
        + mixing * (1.0 - mixing) * (first - running_mean) ** 2
    )
    weights = live_mask / (1.0 + (intensity - blended[:, None]) ** 2 / spread[:, None])
    return (stokes, weights)


def solution(mesh):
    return jax.shard_map(
        local,
        mesh=mesh,
        in_specs=(
            P(None, None, "freq", "tm"),
            P(),
            P(),
            P("freq"),
            P("tm", None, None),
            P("tm", None, None),
        ),
        out_specs=(P("tm", "freq", None, None, None, None), P("tm", "freq", None, None)),
        check_vma=False,
    )
```

time: 1040 us -> 336 us (0.32); the launches traced: 1020 us -> 335 us
  waiting for transfers between devices: 782 us -> 233 us
  blocking collectives: 156 us -> 54 us
  other arithmetic: 24.4 us -> 3.17 us
  between operations: 19.4 us -> 0.78 us
  Pallas kernels: 0 us -> 11.3 us
    psum x1 -> x0, waiting for transfers between devices: 610 us -> none  [local(): lax.psum((first_sum, second_sum, live_count), 'freq')]
    psum x1 -> x0, blocking collectives: 156 us -> none  [local(): lax.psum((first_sum, second_sum, live_count), 'freq')]
    all_to_all x1 -> x2, waiting for transfers between devices: 172 us -> 233 us  [the longest x1 186 us: local(): lax.all_to_all(voltages, BOTH, split_axis=0, concat_axis=0, tiled=True)]
    all_to_all x0 -> x2, blocking collectives: none -> 54 us  [the longest x1 38.1 us: local(): lax.all_to_all(sent, BOTH, split_axis=0, concat_axis=0, tiled=True)]
    pallas_call x0 -> x1, Pallas kernels: none -> 11.3 us  [correlate(): pl.pallas_call(lambda *refs: correlate_kernel(1.0 / math.sqrt(samples), *...]
    another operation x8 -> x0, other arithmetic: 10.5 us -> none  [the longest x5 8.2 us: local(): jnp.stack(pieces)]
    all_to_all x1 -> x2, starting transfers between devices: 15.5 us -> 23.7 us  [the longest x1 16.7 us: local(): lax.all_to_all(voltages, BOTH, split_axis=0, concat_axis=0, tiled=True)]
  transfers between devices with their start and end apart: 3 -> 2, of which waited for: 2 -> 2; matrix products, arithmetic and copies ran while one was open for 1% -> 1% of each run, Pallas kernels for 0% -> 0%
where the time goes in v1:
time: 336 us; the launch traced here: 335 us
  waiting for transfers between devices  233 us (69%)
  blocking collectives  54 us (16%)
  starting transfers between devices  23.7 us (7%)
  Pallas kernels  11.3 us (3%)
  local copies, waits for them, and re-layouts  9.11 us (3%)
    all_to_all x1, waiting for transfers between devices, local(): lax.all_to_all(voltages, BOTH, split_axis=0, concat_axis=0, tiled=True)  186 us
    all_to_all x1, waiting for transfers between devices, local(): lax.all_to_all(stokes.reshape((slots * mine,) + stokes.shape[2:]), 'tm',...  47.2 us
    all_to_all x1, blocking collectives, local(): lax.all_to_all(sent, BOTH, split_axis=0, concat_axis=0, tiled=True)  38.1 us
    all_to_all x1, starting transfers between devices, local(): lax.all_to_all(voltages, BOTH, split_axis=0, concat_axis=0, tiled=True)  16.7 us
    all_to_all x1, blocking collectives, local(): lax.all_to_all(jnp.broadcast_to(planes, (freq_count,) + planes.shape), 'f...  15.9 us
    pallas_call x1, Pallas kernels, correlate(): pl.pallas_call(lambda *refs: correlate_kernel(1.0 / math.sqrt(samples), *...  11.3 us
    unnamed x15, local copies, waits for them, and re-layouts  7.16 us
    all_to_all x1, starting transfers between devices, local(): lax.all_to_all(stokes.reshape((slots * mine,) + stokes.shape[2:]), 'tm',...  7.02 us
  transfers between devices with their start and end apart: 2, of which 2 were waited for; matrix products, arithmetic and copies ran while one was open for 1% of the time, Pallas kernels for 0%

profile of v1, /device:TPU:1, one launch (start us, length us, event | category | flops | bytes accessed | tf_op | source)
XLA Modules:
  0.0 335.0 jit_solution(14094747909882678624)
XLA Ops:
  0.6 0.0 copy-start.3
  0.6 0.0 copy-start.5
  0.7 0.0 copy-start.4
  0.7 16.7 %all-to-all-start = ((bf16[512,2,16,256]{3,2,1,0:T(8,128)(2,1)}), bf16[512,2,16,256]{3,2,1,0:T(8,128)(2,1)}, u32[]{:S(2)}, u32[]{:S(2)}) async-start(bf16[512,2,16,256]{3,2,1,0:T(8,128)(2,1)} %param.6), calls=%async_computation | async-start | bytes 16777216 | tf_op jit(solution)/shard_map/all_to_all | solution.py:104
  17.3 0.0 copy-done.3
  17.3 0.1 copy.21
  17.4 0.0 copy-done.5
  17.5 0.6 gather_fusion
  18.0 0.0 copy-done.4
  18.0 0.7 convert_reduce_fusion
  18.7 0.2 slice_reduce_fusion
  18.9 185.8 %all-to-all-done = bf16[512,2,16,256]{3,2,1,0:T(8,128)(2,1)} async-done(((bf16[512,2,16,256]{3,2,1,0:T(8,128)(2,1)}), bf16[512,2,16,256]{3,2,1,0:T(8,128)(2,1)}, u32[]{:S(2)}, u32[]{:S(2)}) %all-to-all-start) | async-done | bytes 8388640 | tf_op jit(solution)/shard_map/all_to_all | solution.py:104
  204.7 11.3 %correlate.1 = (f32[4,2,4,2,128,128]{5,4,3,2,1,0:T(8,128)S(1)}, f32[4,2,128,128]{3,2,1,0:T(8,128)S(1)}) custom-call(s32[4]{0:T(128)S(1)} %get-tuple-element.7.refs_0_, s32[4]{0:T(128)S(1)} %get-tuple-element.6.refs_1_, s32[2]{0:T(128)S(1)} %get-tuple-element.9.refs_2_, bf16[4,16,4,2,2,16,256]{6,5,4,3,2,1,0:T(8,128)(2,1)} %bitcast.refs_3_.refs_4_, ...), custom_call_target="tpu_custom_call" | custom-call | flops 4294967296 | bytes 33554432 | tf_op jit(solution)/shard_map/correlate/pallas_call | solution.py:68
  216.0 0.0 copy-start
  216.0 2.0 copy-done
  218.0 0.3 copy.24
  218.3 0.3 copy.31
  218.7 0.7 concatenate.3.clone
  219.4 38.1 %all_to_all.20 = f32[256,5,128]{2,1,0:T(8,128)S(1)} all-to-all(f32[256,5,128]{2,1,0:T(8,128)S(1)} %concatenate.3.clone), channel_id=1, replica_groups=mesh['freq'=64,'tm'=4] {'freq','tm'}, dimensions={0} | all-to-all | bytes 1310720 | tf_op jit(solution)/shard_map/all_to_all | solution.py:123
  257.5 0.3 reduce_sum.19
  257.9 15.9 %all_to_all.21 = f32[64,4,128]{2,1,0:T(4,128)S(1)} all-to-all(f32[64,4,128]{2,1,0:T(4,128)S(1)} %broadcast_in_dim.5), channel_id=1, replica_groups=mesh['freq'=64,'tm'=4] {'freq'}, dimensions={0} | all-to-all | bytes 262144 | tf_op jit(solution)/shard_map/all_to_all | solution.py:129
  273.7 0.0 copy-start.1
  273.7 0.0 copy-start.2
  273.7 7.0 %all-to-all-start.1 = ((f32[8,4,2,128,128]{4,3,2,1,0:T(8,128)}), f32[8,4,2,128,128]{4,3,2,1,0:T(8,128)}, u32[]{:S(2)}, u32[]{:S(2)}) async-start(f32[8,4,2,128,128]{4,3,2,1,0:T(8,128)} %bitcast.54), calls=%async_computation.1 | async-start | bytes 8388608 | tf_op jit(solution)/shard_map/all_to_all | solution.py:111
  280.8 0.1 copy.27
  280.8 0.1 copy.28
  280.9 0.0 copy-done.1
  280.9 0.0 copy-done.2
  281.0 47.2 %all-to-all-done.1 = f32[8,4,2,128,128]{4,3,2,1,0:T(8,128)} async-done(((f32[8,4,2,128,128]{4,3,2,1,0:T(8,128)}), f32[8,4,2,128,128]{4,3,2,1,0:T(8,128)}, u32[]{:S(2)}, u32[]{:S(2)}) %all-to-all-start.1) | async-done | bytes 4194336 | tf_op jit(solution)/shard_map/all_to_all | solution.py:111
  328.2 2.2 fusion.7
  330.3 4.7 %copy.33 = f32[1,8,4,2,128,128]{5,4,3,2,1,0:T(8,128)} copy(f32[1,8,4,2,128,128]{5,4,3,2,1,0:T(8,128)} %bitcast.2) | data formatting | bytes 8388608
  (9 shorter events, 0.1 us)
Async XLA Ops:
  0.6 16.7 %copy-start.3 = (s32[4,2]{0,1:T(2,128)S(1)}, s32[4,2]{0,1:T(2,128)}, u32[]{:S(2)}) copy-start(s32[4,2]{0,1:T(2,128)} %param.7) | copy-start | bytes 100
  0.6 16.8 %copy-start.5 = (s32[4]{0:T(128)S(1)}, s32[4]{0:T(128)}, u32[]{:S(2)}) copy-start(s32[4]{0:T(128)} %param.8) | copy-start | bytes 52
  0.7 17.4 %copy-start.4 = (s32[8]{0:T(128)S(1)}, s32[8]{0:T(128)}, u32[]{:S(2)}) copy-start(s32[8]{0:T(128)} %param.9) | copy-start | bytes 100
  0.7 204.0 %all-to-all-start = ((bf16[512,2,16,256]{3,2,1,0:T(8,128)(2,1)}), bf16[512,2,16,256]{3,2,1,0:T(8,128)(2,1)}, u32[]{:S(2)}, u32[]{:S(2)}) async-start(bf16[512,2,16,256]{3,2,1,0:T(8,128)(2,1)} %param.6), calls=%async_computation | async-start | bytes 16777216 | tf_op jit(solution)/shard_map/all_to_all | solution.py:104
  216.0 2.0 copy-start
  273.7 7.2 %copy-start.1 = (f32[1,128,128]{2,1,0:T(8,128)S(1)}, f32[1,128,128]{2,1,0:T(8,128)}, u32[]{:S(2)}) copy-start(f32[1,128,128]{2,1,0:T(8,128)} %param.10) | copy-start | bytes 196612
  273.7 7.2 %copy-start.2 = (f32[1,128,128]{2,1,0:T(8,128)S(1)}, f32[1,128,128]{2,1,0:T(8,128)}, u32[]{:S(2)}) copy-start(f32[1,128,128]{2,1,0:T(8,128)} %param.11) | copy-start | bytes 196612
  273.7 54.4 %all-to-all-start.1 = ((f32[8,4,2,128,128]{4,3,2,1,0:T(8,128)}), f32[8,4,2,128,128]{4,3,2,1,0:T(8,128)}, u32[]{:S(2)}, u32[]{:S(2)}) async-start(f32[8,4,2,128,128]{4,3,2,1,0:T(8,128)} %bitcast.54), calls=%async_computation.1 | async-start | bytes 8388608 | tf_op jit(solution)/shard_map/all_to_all | solution.py:111

commit v2 on v0

v2 whole, which is shorter than its diff:
```python
import math

import jax
import jax.numpy as jnp
from jax import lax
from jax.experimental import pallas as pl
from jax.experimental.pallas import tpu as pltpu
from jax.sharding import Mesh, PartitionSpec as P

BLOCK = 128
mixing = 0.25

FREQ = ("y", "xh", "z")
TM = ("xl", "core")
ALL = FREQ + TM
SHAPE = (4, 2, 8, 2, 2)
SLOTS = 4
FREQS = 64
MINE = 2
BAND = BLOCK // 4
PIECE = (MINE, 4, 2, BLOCK, BLOCK)


def nt(left, right):
    return lax.dot_general(
        left, right, (((1,), (1,)), ((), ())), preferred_element_type=jnp.float32
    )


def correlate_kernel(scale, ids, turned_ref, *refs):
    outs, moment_ref, stage, sems = refs[:SLOTS], refs[SLOTS], refs[SLOTS + 1], refs[SLOTS + 2]
    channel, step = pl.program_id(0), pl.program_id(1)
    _, per_block, pieces, _, _, signals, depth = turned_ref.shape
    width = per_block * signals

    def side(block, part):
        return [
            turned_ref[block, :, piece, 0, part].reshape(width, depth) for piece in range(pieces)
        ]

    row, col = ids[step], ids[SLOTS + step]
    row_re, row_im = side(row, 0), side(row, 1)
    columns = jnp.concatenate(side(col, 0) + side(col, 1), axis=1)
    rows = jnp.concatenate(
        [
            jnp.concatenate(row_re + row_im, axis=1),
            jnp.concatenate(row_im + [-part for part in row_re], axis=1),
        ],
        axis=0,
    )
    both = nt(rows, columns) * scale
    low, high = slice(0, BLOCK), slice(BLOCK, 2 * BLOCK)
    real, imag = both[:width], both[width:]
    i_re = real[low, low] + real[high, high]
    i_im = imag[low, low] + imag[high, high]
    stage[step, channel, 0, 0] = i_re
    stage[step, channel, 0, 1] = i_im
    stage[step, channel, 1, 0] = real[low, low] - real[high, high]
    stage[step, channel, 1, 1] = imag[low, low] - imag[high, high]
    stage[step, channel, 2, 0] = real[low, high] + real[high, low]
    stage[step, channel, 2, 1] = imag[low, high] + imag[high, low]
    stage[step, channel, 3, 0] = imag[low, high] - imag[high, low]
    stage[step, channel, 3, 1] = real[high, low] - real[low, high]

    def copy(number, index):
        return pltpu.make_async_copy(
            stage.at[number, index], outs[number].at[index], sems.at[number, index]
        )

    for number in range(SLOTS):
        for index in range(MINE):

            @pl.when((step == number) & (channel == index))
            def _():
                copy(number, index).start()

    power = i_re * i_re + i_im * i_im
    masked = power * ids[3 * SLOTS + channel].astype(jnp.float32)
    slot = ids[2 * SLOTS + step]
    for order, plane in enumerate((masked, masked * power)):

        @pl.when(channel == 0)
        def _():
            moment_ref[slot, order] = plane

        @pl.when(channel > 0)
        def _():
            moment_ref[slot, order] += plane

    @pl.when((step == SLOTS - 1) & (channel == MINE - 1))
    def _():
        for number in range(SLOTS):
            for index in range(MINE):
                copy(number, index).wait()


def correlate(ids, turned, samples):
    blocks, per_block, pieces, channels, _, signals, depth = turned.shape
    block = (blocks, per_block, pieces, 1, 2, signals, depth)
    moments = (SLOTS, 2, BLOCK, BLOCK)
    return pl.pallas_call(
        lambda *refs: correlate_kernel(1.0 / math.sqrt(samples), *refs),
        grid_spec=pltpu.PrefetchScalarGridSpec(
            num_scalar_prefetch=1,
            grid=(channels, SLOTS),
            in_specs=[pl.BlockSpec(block, lambda c, k, ids: (0, 0, 0, c, 0, 0, 0))],
            out_specs=[pl.BlockSpec(memory_space=pl.ANY)] * SLOTS
            + [pl.BlockSpec(moments, lambda c, k, ids: (0,) * 4)],
            scratch_shapes=[
                pltpu.VMEM((SLOTS,) + PIECE, jnp.float32),
                pltpu.SemaphoreType.DMA((SLOTS, MINE)),
            ],
        ),
        out_shape=[jax.ShapeDtypeStruct(PIECE, jnp.float32)] * SLOTS
        + [jax.ShapeDtypeStruct(moments, jnp.float32)],
        compiler_params=pltpu.CompilerParams(vmem_limit_bytes=32 << 20),
        cost_estimate=pl.CostEstimate(
            flops=SLOTS * channels * 8 * (2 * BLOCK) ** 2 * samples,
            bytes_accessed=13 << 20,
            transcendentals=0,
        ),
        name="correlate",
    )(ids, turned)


def finish_kernel(ids, mask, count_ref, planes_ref, mean_ref, var_ref, *refs):
    pieces, (stokes_ref, weight_ref, sems) = refs[:SLOTS], refs[SLOTS:]
    copies = []
    for number in range(SLOTS):
        first_row = MINE * ids[2 * SLOTS + number]
        placed = pltpu.make_async_copy(
            pieces[number], stokes_ref.at[0, pl.ds(first_row, MINE)], sems.at[number]
        )
        placed.start()
        copies.append(placed)
    count = jnp.sum(count_ref[...], axis=0, keepdims=True)
    for band in range(BLOCK // BAND):
        rows = slice(band * BAND, (band + 1) * BAND)
        first = planes_ref[0, rows] / count
        second = planes_ref[1, rows] / count
        mean = mean_ref[0, rows]
        blended = (1.0 - mixing) * mean + mixing * first
        spread = (
            (1.0 - mixing) * var_ref[0, rows]
            + mixing * (second - first * first)
            + mixing * (1.0 - mixing) * (first - mean) ** 2
        )
        for number in range(SLOTS):
            for index in range(MINE):
                place = MINE * ids[2 * SLOTS + number] + index
                live = mask[place].astype(jnp.float32)
                i_re, i_im = pieces[number][index, 0, 0, rows], pieces[number][index, 0, 1, rows]
                off = i_re * i_re + i_im * i_im - blended
                weight_ref[0, place, rows] = live / (1.0 + off * off / spread)
    for placed in copies:
        placed.wait()


def finish(ids, mask, count, planes, mean, var, pieces):
    whole = pl.BlockSpec(memory_space=pltpu.VMEM)
    scalars = pl.BlockSpec(memory_space=pltpu.SMEM)
    return pl.pallas_call(
        finish_kernel,
        in_specs=[scalars] * 2 + [whole] * (4 + SLOTS),
        out_specs=[pl.BlockSpec(memory_space=pltpu.HBM), whole],
        out_shape=[
            jax.ShapeDtypeStruct((1, MINE * SLOTS, 4, 2, BLOCK, BLOCK), jnp.float32),
            jax.ShapeDtypeStruct((1, MINE * SLOTS, BLOCK, BLOCK), jnp.float32),
        ],
        scratch_shapes=[pltpu.SemaphoreType.DMA((SLOTS,))],
        compiler_params=pltpu.CompilerParams(vmem_limit_bytes=32 << 20),
        cost_estimate=pl.CostEstimate(flops=1 << 21, bytes_accessed=8 << 20, transcendentals=0),
        name="finish",
    )(ids, mask, count, planes, mean, var, *pieces)


def swap(value, names, size, step):
    return lax.ppermute(value, names, [(i, i ^ step) for i in range(size)])


def exchange(value, names):
    return lax.all_to_all(value, names, split_axis=0, concat_axis=0, tiled=True)


def local(voltages, pattern, owner_map, channel_mask, running_mean, running_var):
    total, _, signals, depth = voltages.shape
    own = lax.axis_index(TM)
    slots = jnp.arange(SLOTS, dtype=jnp.int32)
    order = own ^ slots
    tiles = jnp.sum(jnp.where(order[:, None] == slots[None], owner_map[None], 0), axis=1)
    corners = jnp.sum(jnp.where((tiles[:, None] == slots[None])[..., None], pattern[None], 0), axis=1)
    lives = jnp.sum(
        jnp.where(own == slots[:, None], channel_mask.reshape(SLOTS, MINE), 0), axis=0
    )
    ids = jnp.concatenate([corners[:, 0], corners[:, 1], order, lives]).astype(jnp.int32)

    turned = exchange(voltages, ALL)
    turned = turned.reshape(4, FREQS // 4, SLOTS, MINE, 2, signals, depth)
    *pieces, moments = correlate(ids, turned, depth * SLOTS)

    pieces = [pieces[0]] + [swap(pieces[step], TM, SLOTS, step) for step in range(1, SLOTS)]

    rows = BLOCK // FREQS
    part = moments.reshape(SLOTS, 2, FREQS, rows, BLOCK).transpose(2, 0, 1, 3, 4)
    part = jnp.sum(exchange(part.reshape(FREQS * SLOTS, 2 * rows, BLOCK), ALL), axis=0)
    live = jnp.full((1, BLOCK), jnp.sum(channel_mask).astype(jnp.float32))
    part = jnp.concatenate([part, live], axis=0)
    parts = exchange(jnp.broadcast_to(part, (FREQS,) + part.shape), FREQ)
    planes = parts[:, : 2 * rows].reshape(FREQS, 2, rows, BLOCK).transpose(1, 0, 2, 3)
    planes = planes.reshape(2, BLOCK, BLOCK)
    count = parts[:, 2 * rows]
    return tuple(
        finish(ids, channel_mask, count, planes, running_mean, running_var, pieces)
    )


def solution(mesh):
    torus = Mesh(mesh.devices.reshape(SHAPE), ALL)
    return jax.shard_map(
        local,
        mesh=torus,
        in_specs=(
            P(None, None, FREQ, TM),
            P(),
            P(),
            P(FREQ),
            P(TM, None, None),
            P(TM, None, None),
        ),
        out_specs=(P(TM, FREQ, None, None, None, None), P(TM, FREQ, None, None)),
        check_vma=False,
    )
```

time: 1040 us -> 290 us (0.28); the launches traced: 1020 us -> 289 us
  waiting for transfers between devices: 782 us -> 201 us
  blocking collectives: 156 us -> 37.8 us
  other arithmetic: 24.4 us -> 2.6 us
  between operations: 19.4 us -> 1.44 us
  Pallas kernels: 0 us -> 15.3 us
  starting transfers between devices: 15.6 us -> 28.2 us
  local copies, waits for them, and re-layouts: 15.1 us -> 2.69 us
    psum x1 -> x0, waiting for transfers between devices: 610 us -> none  [local(): lax.psum((first_sum, second_sum, live_count), 'freq')]
    psum x1 -> x0, blocking collectives: 156 us -> none  [local(): lax.psum((first_sum, second_sum, live_count), 'freq')]
    all_to_all x0 -> x1, blocking collectives: none -> 37.8 us  [exchange(): return lax.all_to_all(value, names, split_axis=0, concat_axis=0, tiled=True)]
    all_to_all x1 -> x2, waiting for transfers between devices: 172 us -> 201 us  [exchange(): return lax.all_to_all(value, names, split_axis=0, concat_axis=0, tiled=True)]
    pallas_call x0 -> x2, Pallas kernels: none -> 15.3 us  [the longest x1 11.1 us: correlate(): pl.pallas_call(lambda *refs: correlate_kernel(1.0 / math.sqrt(samples), *...]
    another operation x8 -> x0, other arithmetic: 10.5 us -> none  [the longest x5 8.2 us: local(): jnp.stack(pieces)]
    all_to_all x1 -> x2, starting transfers between devices: 15.5 us -> 24.1 us  [exchange(): return lax.all_to_all(value, names, split_axis=0, concat_axis=0, tiled=True)]
  transfers between devices with their start and end apart: 3 -> 5, of which waited for: 2 -> 2; matrix products, arithmetic and copies ran while one was open for 1% -> 1% of each run, Pallas kernels for 0% -> 0%
where the time goes in v2:
time: 290 us; the launch traced here: 289 us
  waiting for transfers between devices  201 us (69%)
  blocking collectives  37.8 us (13%)
  starting transfers between devices  28.2 us (10%)
  Pallas kernels  15.3 us (5%)
    all_to_all x2, waiting for transfers between devices, exchange(): return lax.all_to_all(value, names, split_axis=0, concat_axis=0, tiled=True)  201 us
    all_to_all x1, blocking collectives, exchange(): return lax.all_to_all(value, names, split_axis=0, concat_axis=0, tiled=True)  37.8 us
    all_to_all x2, starting transfers between devices, exchange(): return lax.all_to_all(value, names, split_axis=0, concat_axis=0, tiled=True)  24.1 us
    pallas_call x1, Pallas kernels, correlate(): pl.pallas_call(lambda *refs: correlate_kernel(1.0 / math.sqrt(samples), *...  11.1 us
  transfers between devices with their start and end apart: 5, of which 2 were waited for; matrix products, arithmetic and copies ran while one was open for 1% of the time, Pallas kernels for 0%

profile of v2, /device:TPU:1, one launch (start us, length us, event | category | flops | bytes accessed | tf_op | source)
XLA Modules:
  0.0 289.5 jit_solution(5050654176238925373)
XLA Ops:
  0.6 0.0 copy-start.2
  0.6 0.0 copy-start.6
  0.7 0.0 copy-start.5
  0.7 16.7 %all-to-all-start = ((bf16[512,2,16,256]{3,2,1,0:T(8,128)(2,1)}), bf16[512,2,16,256]{3,2,1,0:T(8,128)(2,1)}, u32[]{:S(2)}, u32[]{:S(2)}) async-start(bf16[512,2,16,256]{3,2,1,0:T(8,128)(2,1)} %param.6), calls=%async_computation | async-start | bytes 16777216 | tf_op jit(solution)/shard_map/all_to_all | solution.py:182
  17.3 0.0 copy-done.2
  17.3 0.1 reshape.54
  17.4 0.0 copy-done.6
  17.4 0.2 select_reduce_fusion.2
  17.6 0.1 iota_compare_fusion
  17.7 0.0 copy-done.5
  17.7 0.1 select_reduce_fusion
  17.9 0.1 select_reduce_fusion.1
  17.9 0.1 pad_add_fusion.refs_0_.ids
  18.0 186.6 %all-to-all-done = bf16[512,2,16,256]{3,2,1,0:T(8,128)(2,1)} async-done(((bf16[512,2,16,256]{3,2,1,0:T(8,128)(2,1)}), bf16[512,2,16,256]{3,2,1,0:T(8,128)(2,1)}, u32[]{:S(2)}, u32[]{:S(2)}) %all-to-all-start) | async-done | bytes 8388640 | tf_op jit(solution)/shard_map/all_to_all | solution.py:182
  204.7 0.0 copy-start
  204.7 0.0 copy-start.1
  204.7 11.1 %correlate.1 = (f32[2,4,2,128,128]{4,3,2,1,0:T(8,128)S(1)}, f32[2,4,2,128,128]{4,3,2,1,0:T(8,128)}, f32[2,4,2,128,128]{4,3,2,1,0:T(8,128)S(1)}, f32[2,4,2,128,128]{4,3,2,1,0:T(8,128)S(1)}, f32[4,2,128,128]{3,2,1,0:T(8,128)S(1)}) custom-call(s32[14]{0:T(128)S(1)} %pad_add_fusion.refs_0_.ids, bf16[4,16,4,2,2,16,256]{6,5,4,3,2,1,0:T(8,128)(2,1)} %bitcast.2.refs_1_), custom_call_target="tpu_custom_call" | custom-call | flops 4294967296 | bytes 13631488 | tf_op jit(solution)/shard_map/correlate/pallas_call | solution.py:101
  215.8 0.0 copy-start.4
  215.8 1.0 copy-done.4
  216.7 0.0 copy-start.3
  216.7 0.3 copy.18
  217.1 1.1 copy.19
  218.2 7.4 %all-to-all-start.1 = ((f32[256,4,128]{2,1,0:T(4,128)}), f32[256,4,128]{2,1,0:T(4,128)}, u32[]{:S(2)}, u32[]{:S(2)}) async-start(f32[256,4,128]{2,1,0:T(4,128)} %copy.19), calls=%async_computation.1 | async-start | bytes 1048576 | tf_op jit(solution)/shard_map/all_to_all | solution.py:182
  225.6 0.0 copy-done.3
  225.6 2.4 collective-permute-start
  228.1 0.0 collective-permute-start.1
  228.1 1.7 collective-permute-start.2
  229.8 0.7 reduce_sum.49
  231.2 14.8 %all-to-all-done.1 = f32[256,4,128]{2,1,0:T(4,128)} async-done(((f32[256,4,128]{2,1,0:T(4,128)}), f32[256,4,128]{2,1,0:T(4,128)}, u32[]{:S(2)}, u32[]{:S(2)}) %all-to-all-start.1) | async-done | bytes 524320 | tf_op jit(solution)/shard_map/all_to_all | solution.py:182
  245.9 1.3 reduce_sum.48
  247.3 37.8 %all_to_all.15 = f32[64,5,128]{2,1,0:T(8,128)S(1)} all-to-all(f32[64,5,128]{2,1,0:T(8,128)S(1)} %broadcast_in_dim.63), channel_id=1, replica_groups=mesh['y'=4,'xh'=2,'z'=8,'xl'=2,'core'=2] {'y','xh','z'}, dimensions={0} | all-to-all | bytes 327680 | tf_op jit(solution)/shard_map/all_to_all | solution.py:182
  285.2 0.0 collective-permute-done.refs_1_
  285.3 0.0 collective-permute-done.1.refs_2_
  285.3 0.0 collective-permute-done.2.refs_3_
  285.3 0.0 copy-done
  285.3 0.0 copy-done.1
  285.3 4.2 %finish.1 = (f32[1,8,4,2,128,128]{5,4,3,2,1,0:T(8,128)}, f32[1,8,128,128]{3,2,1,0:T(8,128)}) custom-call(s32[14]{0:T(128)S(1)} %pad_add_fusion.refs_0_.ids, s32[8]{0:T(128)S(1)} %copy-done.2, f32[64,128]{1,0:T(8,128)S(1)} %bitcast.18, f32[2,128,128]{2,1,0:T(8,128)S(1)} %bitcast.16, f32[1,128,128]{2,1,0:T(8,128)S(1)} %copy-done, ...), custom_call_target="tpu_custom_call" | custom-call | flops 2097152 | bytes 8388608 | tf_op jit(solution)/shard_map/finish/pallas_call | solution.py:162
  (8 shorter events, 0.1 us)
Async XLA Ops:
  0.6 16.7 %copy-start.2 = (s32[8]{0:T(128)S(1)}, s32[8]{0:T(128)}, u32[]{:S(2)}) copy-start(s32[8]{0:T(128)} %mask.1) | copy-start | bytes 100
  0.6 16.8 %copy-start.6 = (s32[4]{0:T(128)S(1)}, s32[4]{0:T(128)}, u32[]{:S(2)}) copy-start(s32[4]{0:T(128)} %param.8) | copy-start | bytes 52
  0.7 17.1 %copy-start.5 = (s32[4,2]{0,1:T(2,128)S(1)}, s32[4,2]{0,1:T(2,128)}, u32[]{:S(2)}) copy-start(s32[4,2]{0,1:T(2,128)} %param.7) | copy-start | bytes 100
  0.7 204.0 %all-to-all-start = ((bf16[512,2,16,256]{3,2,1,0:T(8,128)(2,1)}), bf16[512,2,16,256]{3,2,1,0:T(8,128)(2,1)}, u32[]{:S(2)}, u32[]{:S(2)}) async-start(bf16[512,2,16,256]{3,2,1,0:T(8,128)(2,1)} %param.6), calls=%async_computation | async-start | bytes 16777216 | tf_op jit(solution)/shard_map/all_to_all | solution.py:182
  204.7 80.6 %copy-start = (f32[1,128,128]{2,1,0:T(8,128)S(1)}, f32[1,128,128]{2,1,0:T(8,128)}, u32[]{:S(2)}) copy-start(f32[1,128,128]{2,1,0:T(8,128)} %mean_ref.1) | copy-start | bytes 196612
  204.7 80.6 %copy-start.1 = (f32[1,128,128]{2,1,0:T(8,128)S(1)}, f32[1,128,128]{2,1,0:T(8,128)}, u32[]{:S(2)}) copy-start(f32[1,128,128]{2,1,0:T(8,128)} %var_ref.1) | copy-start | bytes 196612
  215.8 1.0 copy-start.4
  216.7 8.9 %copy-start.3 = (f32[2,4,2,128,128]{4,3,2,1,0:T(8,128)}, f32[2,4,2,128,128]{4,3,2,1,0:T(8,128)S(1)}, u32[]{:S(2)}) copy-start(f32[2,4,2,128,128]{4,3,2,1,0:T(8,128)S(1)} %get-tuple-element.11) | copy-start | bytes 3145732
  218.2 27.7 %all-to-all-start.1 = ((f32[256,4,128]{2,1,0:T(4,128)}), f32[256,4,128]{2,1,0:T(4,128)}, u32[]{:S(2)}, u32[]{:S(2)}) async-start(f32[256,4,128]{2,1,0:T(4,128)} %copy.19), calls=%async_computation.1 | async-start | bytes 1048576 | tf_op jit(solution)/shard_map/all_to_all | solution.py:182
  225.6 59.6 %collective-permute-start = (f32[2,4,2,128,128]{4,3,2,1,0:T(8,128)}, f32[2,4,2,128,128]{4,3,2,1,0:T(8,128)S(1)}, u32[]{:S(2)}, u32[]{:S(2)}) collective-permute-start(f32[2,4,2,128,128]{4,3,2,1,0:T(8,128)} %get-tuple-element.9), channel_id=1, source_target_pairs={{0,1},{1,0},{2,3},{3,2},{4,5},{5,4},{6,7},{7,6},{8,9},{9,8},{10,11... | collective-permute-start | bytes 3145736 | tf_op jit(solution)/shard_map/ppermute | solution.py:178
  228.1 57.2 %collective-permute-start.1 = (f32[2,4,2,128,128]{4,3,2,1,0:T(8,128)}, f32[2,4,2,128,128]{4,3,2,1,0:T(8,128)S(1)}, u32[]{:S(2)}, u32[]{:S(2)}) collective-permute-start(f32[2,4,2,128,128]{4,3,2,1,0:T(8,128)} %copy-done.4), channel_id=1, source_target_pairs={{0,2},{1,3},{2,0},{3,1},{4,6},{5,7},{6,4},{7,5},{8,10},{9,11},{10,... | collective-permute-start | bytes 3145736 | tf_op jit(solution)/shard_map/ppermute | solution.py:178
  228.1 57.2 %collective-permute-start.2 = (f32[2,4,2,128,128]{4,3,2,1,0:T(8,128)}, f32[2,4,2,128,128]{4,3,2,1,0:T(8,128)}, u32[]{:S(2)}, u32[]{:S(2)}) collective-permute-start(f32[2,4,2,128,128]{4,3,2,1,0:T(8,128)} %copy-done.3), channel_id=1, source_target_pairs={{0,3},{1,2},{2,1},{3,0},{4,7},{5,6},{6,5},{7,4},{8,11},{9,10},{10,... | collective-permute-start | bytes 3145736 | tf_op jit(solution)/shard_map/ppermute | solution.py:178

commit v3 on v2

v3 whole, which is shorter than its diff:
```python
import math

import jax
import jax.numpy as jnp
from jax import lax
from jax.experimental import pallas as pl
from jax.experimental.pallas import tpu as pltpu
from jax.sharding import Mesh, PartitionSpec as P

BLOCK = 128
mixing = 0.25

FREQ = ("y", "xh", "z")
TM = ("xl", "core")
ALL = FREQ + TM
SHAPE = (4, 2, 8, 2, 2)
SLOTS = 4
FREQS = 64
MINE = 2
BAND = BLOCK // 4
PLANES = (4, 2, BLOCK, BLOCK)
PARTS = ((0, 0, 2), (1, 0, 2), (2, 0, 2), (3, 0, 1), (3, 1, 1))


def nt(left, right):
    return lax.dot_general(
        left, right, (((1,), (1,)), ((), ())), preferred_element_type=jnp.float32
    )


def correlate_kernel(scale, ids, turned_ref, *refs):
    outs, moment_ref = refs[: len(PARTS)], refs[len(PARTS)]
    loaded, stage, load_sems, sems = refs[len(PARTS) + 1 :]
    blocks, per_block, pieces, _, _, signals, depth = turned_ref.shape
    width = per_block * signals

    def load(channel, block):
        return pltpu.make_async_copy(
            turned_ref.at[block, :, :, channel], loaded.at[channel, block], load_sems.at[channel, block]
        )

    def copy(number, channel):
        for out, (step, first, many) in zip(outs, PARTS):
            if step == number and first <= channel < first + many:
                return pltpu.make_async_copy(
                    stage.at[number, channel], out.at[channel - first], sems.at[number, channel]
                )

    def side(channel, block, part):
        return [
            loaded[channel, block, :, piece, part].reshape(width, depth) for piece in range(pieces)
        ]

    for channel in range(MINE):
        for block in range(blocks):
            load(channel, block).start()
    low, high = slice(0, BLOCK), slice(BLOCK, 2 * BLOCK)
    for channel in range(MINE):
        live = ids[3 * SLOTS + channel].astype(jnp.float32)
        for block in range(blocks):
            load(channel, block).wait()
        for number in range(SLOTS):
            row, col, slot = ids[number], ids[SLOTS + number], ids[2 * SLOTS + number]
            row_re, row_im = side(channel, row, 0), side(channel, row, 1)
            columns = jnp.concatenate(side(channel, col, 0) + side(channel, col, 1), axis=1)
            real = nt(jnp.concatenate(row_re + row_im, axis=1), columns) * scale
            minus_re = [-part for part in row_re]
            imag = nt(jnp.concatenate(row_im + minus_re, axis=1), columns) * scale
            i_re = real[low, low] + real[high, high]
            i_im = imag[low, low] + imag[high, high]
            stage[number, channel, 0, 0] = i_re
            stage[number, channel, 0, 1] = i_im
            stage[number, channel, 1, 0] = real[low, low] - real[high, high]
            stage[number, channel, 1, 1] = imag[low, low] - imag[high, high]
            stage[number, channel, 2, 0] = real[low, high] + real[high, low]
            stage[number, channel, 2, 1] = imag[low, high] + imag[high, low]
            stage[number, channel, 3, 0] = imag[low, high] - imag[high, low]
            stage[number, channel, 3, 1] = real[high, low] - real[low, high]
            copy(number, channel).start()
            power = i_re * i_re + i_im * i_im
            masked = power * live
            for order, plane in enumerate((masked, masked * power)):
                if channel > 0:
                    plane = plane + moment_ref[slot, order]
                moment_ref[slot, order] = plane
    for channel in range(MINE):
        for number in range(SLOTS):
            copy(number, channel).wait()


def correlate(ids, turned, samples):
    blocks, per_block, pieces, channels, _, signals, depth = turned.shape
    anywhere = pl.BlockSpec(memory_space=pl.ANY)
    return pl.pallas_call(
        lambda *refs: correlate_kernel(1.0 / math.sqrt(samples), *refs),
        in_specs=[pl.BlockSpec(memory_space=pltpu.SMEM), anywhere],
        out_specs=[anywhere] * len(PARTS) + [pl.BlockSpec(memory_space=pltpu.VMEM)],
        scratch_shapes=[
            pltpu.VMEM((channels, blocks, per_block, pieces, 2, signals, depth), turned.dtype),
            pltpu.VMEM((SLOTS, channels) + PLANES, jnp.float32),
            pltpu.SemaphoreType.DMA((channels, blocks)),
            pltpu.SemaphoreType.DMA((SLOTS, channels)),
        ],
        out_shape=[jax.ShapeDtypeStruct((many,) + PLANES, jnp.float32) for _, _, many in PARTS]
        + [jax.ShapeDtypeStruct((SLOTS, 2, BLOCK, BLOCK), jnp.float32)],
        compiler_params=pltpu.CompilerParams(vmem_limit_bytes=16 << 20),
        cost_estimate=pl.CostEstimate(
            flops=SLOTS * channels * 8 * (2 * BLOCK) ** 2 * samples,
            bytes_accessed=13 << 20,
            transcendentals=0,
        ),
        name="correlate",
    )(ids, turned)


def spread_kernel(mask, bands_ref, _, held_ref, passed_ref, part_ref, sem):
    passed = pltpu.make_async_copy(held_ref, passed_ref, sem)
    passed.start()
    total = jnp.sum(bands_ref[...], axis=0)
    live = mask[0]
    for index in range(1, mask.shape[0]):
        live = live + mask[index]
    rows = total.shape[0]
    row = jnp.full((1, BLOCK), live.astype(jnp.float32))
    for receiver in range(part_ref.shape[0]):
        part_ref[receiver, :rows] = total
        part_ref[receiver, rows:] = row
    passed.wait()


def spread_sums(mask, bands, earlier, held):
    whole = pl.BlockSpec(memory_space=pltpu.VMEM)
    anywhere = pl.BlockSpec(memory_space=pl.ANY)
    return pl.pallas_call(
        spread_kernel,
        in_specs=[pl.BlockSpec(memory_space=pltpu.SMEM), whole, whole, anywhere],
        out_specs=[whole] * 2,
        out_shape=[
            jax.ShapeDtypeStruct(held.shape, jnp.float32),
            jax.ShapeDtypeStruct((FREQS, bands.shape[1] + 1, BLOCK), jnp.float32),
        ],
        scratch_shapes=[pltpu.SemaphoreType.DMA],
        cost_estimate=pl.CostEstimate(flops=1 << 18, bytes_accessed=1 << 20, transcendentals=0),
        name="spread_sums",
    )(mask, bands, earlier, held)


def finish_kernel(parts, ids, mask, count_ref, planes_ref, mean_ref, var_ref, *refs):
    pieces, (stokes_ref, weight_ref, loaded, stage, sems) = refs[: len(parts)], refs[-5:]
    loads, copies = [], []
    for index, (_, _, many) in enumerate(parts):
        loads.append(
            pltpu.make_async_copy(pieces[index], loaded.at[index, pl.ds(0, many)], sems.at[index, 0])
        )
        loads[-1].start()
    count = jnp.sum(count_ref[...], axis=0, keepdims=True)
    bands = []
    for band in range(BLOCK // BAND):
        rows = slice(band * BAND, (band + 1) * BAND)
        first = planes_ref[0, rows] / count
        second = planes_ref[1, rows] / count
        mean = mean_ref[0, rows]
        blended = (1.0 - mixing) * mean + mixing * first
        spread = (
            (1.0 - mixing) * var_ref[0, rows]
            + mixing * (second - first * first)
            + mixing * (1.0 - mixing) * (first - mean) ** 2
        )
        bands.append((rows, blended, spread))
    for index, (step, start, many) in enumerate(parts):
        place = MINE * ids[2 * SLOTS + step] + start
        span, held = pl.ds(place, many), pl.ds(0, many)
        loads[index].wait()
        copies.append(
            pltpu.make_async_copy(
                loaded.at[index, held], stokes_ref.at[0, span], sems.at[index, 1]
            )
        )
        copies[-1].start()
        for channel in range(many):
            live = mask[place + channel].astype(jnp.float32)
            for rows, blended, spread in bands:
                i_re, i_im = loaded[index, channel, 0, 0, rows], loaded[index, channel, 0, 1, rows]
                off = i_re * i_re + i_im * i_im - blended
                stage[index, channel, rows] = live / (1.0 + off * off / spread)
        copies.append(
            pltpu.make_async_copy(stage.at[index, held], weight_ref.at[0, span], sems.at[index, 2])
        )
        copies[-1].start()
    for copy in copies:
        copy.wait()


def finish(parts, cost, ids, mask, ready, pieces, outs):
    whole = pl.BlockSpec(memory_space=pltpu.VMEM)
    scalars = pl.BlockSpec(memory_space=pltpu.SMEM)
    placed = pl.BlockSpec(memory_space=pltpu.HBM)
    anywhere = pl.BlockSpec(memory_space=pl.ANY)
    count = len(parts)
    return pl.pallas_call(
        lambda *refs: finish_kernel(parts, *refs),
        in_specs=[scalars] * 2
        + [whole] * 4
        + [placed if step == 0 else anywhere for step, _, _ in parts]
        + [placed] * len(outs),
        out_specs=[placed] * 2,
        out_shape=[
            jax.ShapeDtypeStruct((1, MINE * SLOTS) + PLANES, jnp.float32),
            jax.ShapeDtypeStruct((1, MINE * SLOTS, BLOCK, BLOCK), jnp.float32),
        ],
        input_output_aliases={6 + count + index: index for index in range(len(outs))},
        scratch_shapes=[
            pltpu.VMEM((count, MINE) + PLANES, jnp.float32),
            pltpu.VMEM((count, MINE, BLOCK, BLOCK), jnp.float32),
            pltpu.SemaphoreType.DMA((count, 3)),
        ],
        compiler_params=pltpu.CompilerParams(vmem_limit_bytes=16 << 20),
        cost_estimate=pl.CostEstimate(
            flops=cost, bytes_accessed=count << 21, transcendentals=0
        ),
        name=f"finish_{count}",
    )(ids, mask, *ready, *pieces, *outs)


def swap(value, names, size, step):
    return lax.ppermute(value, names, [(i, i ^ step) for i in range(size)])


def exchange(value, names):
    return lax.all_to_all(value, names, split_axis=0, concat_axis=0, tiled=True)


def local(voltages, pattern, owner_map, channel_mask, running_mean, running_var):
    total, _, signals, depth = voltages.shape
    own = lax.axis_index(TM)
    slots = jnp.arange(SLOTS, dtype=jnp.int32)
    order = own ^ slots
    tiles = jnp.sum(jnp.where(order[:, None] == slots[None], owner_map[None], 0), axis=1)
    corners = jnp.sum(jnp.where((tiles[:, None] == slots[None])[..., None], pattern[None], 0), axis=1)
    lives = jnp.sum(
        jnp.where(own == slots[:, None], channel_mask.reshape(SLOTS, MINE), 0), axis=0
    )
    ids = jnp.concatenate([corners[:, 0], corners[:, 1], order, lives]).astype(jnp.int32)

    turned = exchange(voltages, ALL)
    turned = turned.reshape(4, FREQS // 4, SLOTS, MINE, 2, signals, depth)
    *held, moments = correlate(ids, turned, depth * SLOTS)
    pieces = held[:1] + [swap(held[number], TM, SLOTS, number) for number in range(1, SLOTS)]

    rows = BLOCK // FREQS
    part = moments.reshape(SLOTS, 2, FREQS, rows, BLOCK).transpose(2, 0, 1, 3, 4)
    part = exchange(part.reshape(FREQS * SLOTS, 2 * rows, BLOCK), ALL)
    last, part = spread_sums(channel_mask, part, pieces[2], held[4])
    parts = exchange(part, FREQ)
    last = swap(last, TM, SLOTS, 3)
    planes = parts[:, : 2 * rows].reshape(FREQS, 2, rows, BLOCK).transpose(1, 0, 2, 3)
    ready = (parts[:, 2 * rows], planes.reshape(2, BLOCK, BLOCK), running_mean, running_var)
    outs = finish(PARTS[:4], 1 << 33, ids, channel_mask, ready, pieces, [])
    return tuple(finish(PARTS[4:], 1 << 20, ids, channel_mask, ready, [last], outs))


def solution(mesh):
    torus = Mesh(mesh.devices.reshape(SHAPE), ALL)
    return jax.shard_map(
        local,
        mesh=torus,
        in_specs=(
            P(None, None, FREQ, TM),
            P(),
            P(),
            P(FREQ),
            P(TM, None, None),
            P(TM, None, None),
        ),
        out_specs=(P(TM, FREQ, None, None, None, None), P(TM, FREQ, None, None)),
        check_vma=False,
    )
```

time: 290 us -> 280 us (0.966)
  blocking collectives: 37.8 us -> 0 us
  waiting for transfers between devices: 201 us -> 221 us
  starting transfers between devices: 28.2 us -> 33.4 us
  local copies, waits for them, and re-layouts: 2.69 us -> 6.43 us
    all_to_all x1 -> x0, blocking collectives: 37.8 us -> none  [exchange(): return lax.all_to_all(value, names, split_axis=0, concat_axis=0, tiled=True)]
    all_to_all x2 -> x3, waiting for transfers between devices: 201 us -> 221 us  [exchange(): return lax.all_to_all(value, names, split_axis=0, concat_axis=0, tiled=True)]
    all_to_all x2 -> x3, starting transfers between devices: 24.1 us -> 29.9 us  [exchange(): return lax.all_to_all(value, names, split_axis=0, concat_axis=0, tiled=True)]
    unnamed x14 -> x24, local copies, waits for them, and re-layouts: 0.99 us -> 5.24 us
    pallas_call x1 -> x3, Pallas kernels: 4.2 us -> 7.7 us  [the longest x2 4.38 us: finish(): pl.pallas_call(lambda *refs: finish_kernel(parts, *refs), in_specs=[scala...]
  transfers between devices with their start and end apart: 5 -> 7, of which waited for: 2 -> 3; matrix products, arithmetic and copies ran while one was open for 1% -> 1% of each run, Pallas kernels for 0% -> 2%
where the time goes in v3:
time: 280 us; the launch traced here: 279 us
  waiting for transfers between devices  221 us (79%)
  starting transfers between devices  33.4 us (12%)
  Pallas kernels  16.6 us (6%)
  local copies, waits for them, and re-layouts  6.43 us (2%)
    all_to_all x3, waiting for transfers between devices, exchange(): return lax.all_to_all(value, names, split_axis=0, concat_axis=0, tiled=True)  221 us
    all_to_all x3, starting transfers between devices, exchange(): return lax.all_to_all(value, names, split_axis=0, concat_axis=0, tiled=True)  29.9 us
    pallas_call x1, Pallas kernels, correlate(): pl.pallas_call(lambda *refs: correlate_kernel(1.0 / math.sqrt(samples), *...  8.93 us
  transfers between devices with their start and end apart: 7, of which 3 were waited for; matrix products, arithmetic and copies ran while one was open for 1% of the time, Pallas kernels for 2%

profile of v3, /device:TPU:1, one launch (start us, length us, event | category | flops | bytes accessed | tf_op | source)
XLA Modules:
  0.0 279.3 jit_solution(2984919094906160114)
XLA Ops:
  0.6 0.0 copy-start.5
  0.6 0.0 copy-start.11
  0.7 0.0 copy-start.10
  0.7 16.7 %all-to-all-start = ((bf16[512,2,16,256]{3,2,1,0:T(8,128)(2,1)}), bf16[512,2,16,256]{3,2,1,0:T(8,128)(2,1)}, u32[]{:S(2)}, u32[]{:S(2)}) async-start(bf16[512,2,16,256]{3,2,1,0:T(8,128)(2,1)} %param.6), calls=%async_computation | async-start | bytes 16777216 | tf_op jit(solution)/shard_map/all_to_all | solution.py:230
  17.3 0.0 copy-done.5
  17.3 0.1 reshape.54
  17.4 0.0 copy-done.11
  17.4 0.2 select_reduce_fusion.2
  17.6 0.1 iota_compare_fusion
  17.7 0.0 copy-done.10
  17.7 0.1 select_reduce_fusion
  17.9 0.1 select_reduce_fusion.1
  17.9 0.1 pad_add_fusion.refs_0_
  18.0 186.6 %all-to-all-done = bf16[512,2,16,256]{3,2,1,0:T(8,128)(2,1)} async-done(((bf16[512,2,16,256]{3,2,1,0:T(8,128)(2,1)}), bf16[512,2,16,256]{3,2,1,0:T(8,128)(2,1)}, u32[]{:S(2)}, u32[]{:S(2)}) %all-to-all-start) | async-done | bytes 8388640 | tf_op jit(solution)/shard_map/all_to_all | solution.py:230
  204.7 0.0 copy-start.3
  204.7 0.0 copy-start.4
  204.7 0.0 copy-start.6
  204.7 8.9 %correlate.1 = (f32[2,4,2,128,128]{4,3,2,1,0:T(8,128)S(1)}, f32[2,4,2,128,128]{4,3,2,1,0:T(8,128)S(1)}, f32[2,4,2,128,128]{4,3,2,1,0:T(8,128)}, f32[1,4,2,128,12...) custom-call(s32[14]{0:T(128)S(1)} %pad_add_fusion.refs_0_, ...), custom_call_target="tpu_custom_call" | custom-call | flops 4294967296 | bytes 13631488 | tf_op jit(solution)/shard_map/correlate/pallas_call | solution.py:94
  213.6 0.0 copy-start.2
  213.6 0.8 copy-done.2
  214.4 0.0 copy-start.8
  214.4 1.0 copy-done.8
  215.4 0.0 copy-start.7
  215.4 0.0 collective-permute-start
  215.4 1.0 copy.22
  216.4 0.0 copy-done.7
  216.4 7.8 %all-to-all-start.1 = ((f32[256,4,128]{2,1,0:T(4,128)}), f32[256,4,128]{2,1,0:T(4,128)}, u32[]{:S(2)}, u32[]{:S(2)}) async-start(f32[256,4,128]{2,1,0:T(4,128)} %bitcast.21), calls=%async_computation.1 | async-start | bytes 1048576 | tf_op jit(solution)/shard_map/all_to_all | solution.py:230
  224.3 2.3 collective-permute-start.2
  226.6 0.0 collective-permute-start.3
  226.6 22.7 %all-to-all-done.1.bands_ref = f32[256,4,128]{2,1,0:T(4,128)} async-done(((f32[256,4,128]{2,1,0:T(4,128)}), f32[256,4,128]{2,1,0:T(4,128)}, u32[]{:S(2)}, u32[]{:S(2)}) %all-to-all-start.1) | async-done | bytes 524320 | tf_op jit(solution)/shard_map/all_to_all | solution.py:230
  249.3 0.0 collective-permute-done._.refs_8_
  249.3 0.0 copy-start
  249.3 1.0 copy-done
  250.2 3.3 %spread_sums.1 = (f32[1,4,2,128,128]{4,3,2,1,0:T(8,128)}, f32[64,5,128]{2,1,0:T(8,128)}) custom-call(s32[8]{0:T(128)} %refs_1_.3, f32[256,4,128]{2,1,0:T(4,128)} %all-to-all-done.1.bands_ref, f32[2,4,2,128,128]{4,3,2,1,0:T(8,128)} %copy-done, f32[1,4,2,128,128]{4,3,2,1,0:T(8,128)} %copy-done.2), custom_call_target="tpu_custom_call" | custom-call | flops 262144 | bytes 1048576 | tf_op jit(solution)/shard_map/spread_sums/pallas_call | solution.py:134
  253.6 5.4 %all-to-all-start.2 = ((f32[64,5,128]{2,1,0:T(8,128)}), f32[64,5,128]{2,1,0:T(8,128)S(1)}, u32[]{:S(2)}, u32[]{:S(2)}) async-start(f32[64,5,128]{2,1,0:T(8,128)} %get-tuple-element.15), calls=%async_computation.2 | async-start | bytes 524288 | tf_op jit(solution)/shard_map/all_to_all | solution.py:230
  258.9 1.2 collective-permute-start.1
  260.2 12.2 %all-to-all-done.2 = f32[64,5,128]{2,1,0:T(8,128)S(1)} async-done(((f32[64,5,128]{2,1,0:T(8,128)}), f32[64,5,128]{2,1,0:T(8,128)S(1)}, u32[]{:S(2)}, u32[]{:S(2)}) %all-to-all-start.2) | async-done | bytes 163872 | tf_op jit(solution)/shard_map/all_to_all | solution.py:230
  272.4 0.0 collective-permute-done.3.refs_9_
  272.4 0.0 collective-permute-done.2.refs_7_
  272.5 0.0 copy-done.3
  272.5 0.0 copy-done.4
  272.5 0.0 copy-done.6
  272.5 0.0 copy-start.1
  272.5 1.2 copy-done.1
  273.7 1.2 copy-done.9
  274.9 2.9 %finish_4.1 = (f32[1,8,4,2,128,128]{5,4,3,2,1,0:T(8,128)}, f32[1,8,128,128]{3,2,1,0:T(8,128)}) custom-call(s32[14]{0:T(128)S(1)} %pad_add_fusion.refs_0_, s32[8]{0:T(128)S(1)} %copy-done.6, f32[64,128]{1,0:T(8,128)S(1)} %bitcast.19, f32[2,128,128]{2,1,0:T(8,128)S(1)} %bitcast.16, f32[1,128,128]{2,1,0:T(8,128)S(1)} %copy-done.3, ...), custom_call_target="tpu_custom_call" | custom-call | flops 8589934592 | bytes 8388608 | tf_op jit(solution)/shard_map/finish_4/pallas_call | solution.py:200
  277.9 0.0 collective-permute-done.1.refs_6_
  277.9 1.5 finish_1.1
  (7 shorter events, 0.1 us)
Async XLA Ops:
  0.6 16.7 %copy-start.5 = (s32[8]{0:T(128)S(1)}, s32[8]{0:T(128)}, u32[]{:S(2)}) copy-start(s32[8]{0:T(128)} %refs_1_.3) | copy-start | bytes 100
  0.6 16.8 %copy-start.11 = (s32[4]{0:T(128)S(1)}, s32[4]{0:T(128)}, u32[]{:S(2)}) copy-start(s32[4]{0:T(128)} %param.8) | copy-start | bytes 52
  0.7 17.1 %copy-start.10 = (s32[4,2]{0,1:T(2,128)S(1)}, s32[4,2]{0,1:T(2,128)}, u32[]{:S(2)}) copy-start(s32[4,2]{0,1:T(2,128)} %param.7) | copy-start | bytes 100
  0.7 204.0 %all-to-all-start = ((bf16[512,2,16,256]{3,2,1,0:T(8,128)(2,1)}), bf16[512,2,16,256]{3,2,1,0:T(8,128)(2,1)}, u32[]{:S(2)}, u32[]{:S(2)}) async-start(bf16[512,2,16,256]{3,2,1,0:T(8,128)(2,1)} %param.6), calls=%async_computation | async-start | bytes 16777216 | tf_op jit(solution)/shard_map/all_to_all | solution.py:230
  204.7 67.8 %copy-start.3 = (f32[1,128,128]{2,1,0:T(8,128)S(1)}, f32[1,128,128]{2,1,0:T(8,128)}, u32[]{:S(2)}) copy-start(f32[1,128,128]{2,1,0:T(8,128)} %refs_4_.3) | copy-start | bytes 196612
  204.7 67.8 %copy-start.4 = (f32[1,128,128]{2,1,0:T(8,128)S(1)}, f32[1,128,128]{2,1,0:T(8,128)}, u32[]{:S(2)}) copy-start(f32[1,128,128]{2,1,0:T(8,128)} %refs_5_.3) | copy-start | bytes 196612
  204.7 67.8 %copy-start.6 = (s32[8]{0:T(128)S(1)}, s32[8]{0:T(128)}, u32[]{:S(2)}) copy-start(s32[8]{0:T(128)} %refs_1_.3) | copy-start | bytes 100
  213.6 0.8 copy-start.2
  214.4 1.0 copy-start.8
  215.4 1.0 copy-start.7
  215.4 33.8 %collective-permute-start = (f32[2,4,2,128,128]{4,3,2,1,0:T(8,128)}, f32[2,4,2,128,128]{4,3,2,1,0:T(8,128)S(1)}, u32[]{:S(2)}, u32[]{:S(2)}) collective-permute-start(f32[2,4,2,128,128]{4,3,2,1,0:T(8,128)} %get-tuple-element.13), channel_id=1, source_target_pairs={{0,2},{1,3},{2,0},{3,1},{4,6},{5,7},{6,4},{7,5},{8,10},{9,11},{10,... | collective-permute-start | bytes 3145736 | tf_op jit(solution)/shard_map/ppermute | solution.py:226
  216.4 32.8 %all-to-all-start.1 = ((f32[256,4,128]{2,1,0:T(4,128)}), f32[256,4,128]{2,1,0:T(4,128)}, u32[]{:S(2)}, u32[]{:S(2)}) async-start(f32[256,4,128]{2,1,0:T(4,128)} %bitcast.21), calls=%async_computation.1 | async-start | bytes 1048576 | tf_op jit(solution)/shard_map/all_to_all | solution.py:230
  224.3 48.2 %collective-permute-start.2 = (f32[2,4,2,128,128]{4,3,2,1,0:T(8,128)S(1)}, f32[2,4,2,128,128]{4,3,2,1,0:T(8,128)S(1)}, u32[]{:S(2)}, u32[]{:S(2)}) collective-permute-start(f32[2,4,2,128,128]{4,3,2,1,0:T(8,128)S(1)} %get-tuple-element.18), channel_id=1, source_target_pairs={{0,1},{1,0},{2,3},{3,2},{4,5},{5,4},{6,7},{7,6},{8,9},{9,8},{10,11... | collective-permute-start | bytes 3145736 | tf_op jit(solution)/shard_map/ppermute | solution.py:226
  226.6 45.9 %collective-permute-start.3 = (f32[1,4,2,128,128]{4,3,2,1,0:T(8,128)}, f32[1,4,2,128,128]{4,3,2,1,0:T(8,128)}, u32[]{:S(2)}, u32[]{:S(2)}) collective-permute-start(f32[1,4,2,128,128]{4,3,2,1,0:T(8,128)} %copy-done.7), channel_id=1, source_target_pairs={{0,3},{1,2},{2,1},{3,0},{4,7},{5,6},{6,5},{7,4},{8,11},{9,10},{10,... | collective-permute-start | bytes 1572872 | tf_op jit(solution)/shard_map/ppermute | solution.py:226
  249.3 1.0 copy-start
  253.6 18.8 %all-to-all-start.2 = ((f32[64,5,128]{2,1,0:T(8,128)}), f32[64,5,128]{2,1,0:T(8,128)S(1)}, u32[]{:S(2)}, u32[]{:S(2)}) async-start(f32[64,5,128]{2,1,0:T(8,128)} %get-tuple-element.15), calls=%async_computation.2 | async-start | bytes 524288 | tf_op jit(solution)/shard_map/all_to_all | solution.py:230
  258.9 18.9 %collective-permute-start.1 = (f32[1,4,2,128,128]{4,3,2,1,0:T(8,128)}, f32[1,4,2,128,128]{4,3,2,1,0:T(8,128)S(1)}, u32[]{:S(2)}, u32[]{:S(2)}) collective-permute-start(f32[1,4,2,128,128]{4,3,2,1,0:T(8,128)} %get-tuple-element.16), channel_id=1, source_target_pairs={{0,3},{1,2},{2,1},{3,0},{4,7},{5,6},{6,5},{7,4},{8,11},{9,10},{10,... | collective-permute-start | bytes 1572872 | tf_op jit(solution)/shard_map/ppermute | solution.py:226
  272.5 1.2 copy-start.1
  273.7 1.2 copy-start.9

commit v4 on v3

--- a/solution.py
+++ b/solution.py
@@ -103,7 +103,7 @@
         ],
         out_shape=[jax.ShapeDtypeStruct((many,) + PLANES, jnp.float32) for _, _, many in PARTS]
         + [jax.ShapeDtypeStruct((SLOTS, 2, BLOCK, BLOCK), jnp.float32)],
-        compiler_params=pltpu.CompilerParams(vmem_limit_bytes=16 << 20),
+        compiler_params=pltpu.CompilerParams(vmem_limit_bytes=56 << 20),
         cost_estimate=pl.CostEstimate(
             flops=SLOTS * channels * 8 * (2 * BLOCK) ** 2 * samples,
             bytes_accessed=13 << 20,
@@ -133,7 +133,12 @@
     anywhere = pl.BlockSpec(memory_space=pl.ANY)
     return pl.pallas_call(
         spread_kernel,
-        in_specs=[pl.BlockSpec(memory_space=pltpu.SMEM), whole, whole, anywhere],
+        in_specs=[
+            pl.BlockSpec(memory_space=pltpu.SMEM),
+            whole,
+            pl.BlockSpec(memory_space=pltpu.HBM),
+            anywhere,
+        ],
         out_specs=[whole] * 2,
         out_shape=[
             jax.ShapeDtypeStruct(held.shape, jnp.float32),
@@ -145,14 +150,54 @@
     )(mask, bands, earlier, held)
 
 
-def finish_kernel(parts, ids, mask, count_ref, planes_ref, mean_ref, var_ref, *refs):
-    pieces, (stokes_ref, weight_ref, loaded, stage, sems) = refs[: len(parts)], refs[-5:]
+def moving_kernel(parts, ids, *refs):
+    pieces, (stokes_ref, power_ref, loaded, sems) = refs[: len(parts)], refs[len(parts) :]
     loads, copies = [], []
     for index, (_, _, many) in enumerate(parts):
         loads.append(
             pltpu.make_async_copy(pieces[index], loaded.at[index, pl.ds(0, many)], sems.at[index, 0])
         )
         loads[-1].start()
+    for index, (step, start, many) in enumerate(parts):
+        span = pl.ds(MINE * ids[2 * SLOTS + step] + start, many)
+        loads[index].wait()
+        copies.append(
+            pltpu.make_async_copy(
+                loaded.at[index, pl.ds(0, many)], stokes_ref.at[0, span], sems.at[index, 1]
+            )
+        )
+        copies[-1].start()
+        for channel in range(many):
+            i_re, i_im = loaded[index, channel, 0, 0], loaded[index, channel, 0, 1]
+            power_ref[index, channel] = i_re * i_re + i_im * i_im
+    for copy in copies:
+        copy.wait()
+
+
+def place(parts, ids, pieces):
+    placed = pl.BlockSpec(memory_space=pltpu.HBM)
+    count = len(parts)
+    return pl.pallas_call(
+        lambda *refs: moving_kernel(parts, *refs),
+        in_specs=[pl.BlockSpec(memory_space=pltpu.SMEM)] + [placed] * count,
+        out_specs=[placed, pl.BlockSpec(memory_space=pltpu.VMEM)],
+        out_shape=[
+            jax.ShapeDtypeStruct((1, MINE * SLOTS) + PLANES, jnp.float32),
+            jax.ShapeDtypeStruct((count, MINE, BLOCK, BLOCK), jnp.float32),
+        ],
+        scratch_shapes=[
+            pltpu.VMEM((count, MINE) + PLANES, jnp.float32),
+            pltpu.SemaphoreType.DMA((count, 2)),
+        ],
+        compiler_params=pltpu.CompilerParams(vmem_limit_bytes=16 << 20),
+        cost_estimate=pl.CostEstimate(
+            flops=count << 17, bytes_accessed=count << 21, transcendentals=0
+        ),
+        name="place",
+    )(ids, *pieces)
+
+
+def bands_of(count_ref, planes_ref, mean_ref, var_ref):
     count = jnp.sum(count_ref[...], axis=0, keepdims=True)
     bands = []
     for band in range(BLOCK // BAND):
@@ -167,6 +212,60 @@
             + mixing * (1.0 - mixing) * (first - mean) ** 2
         )
         bands.append((rows, blended, spread))
+    return bands
+
+
+def weigh_kernel(parts, ids, mask, count_ref, planes_ref, mean_ref, var_ref, *refs):
+    power_ref, weight_ref, stage, sems = refs
+    copies = []
+    bands = bands_of(count_ref, planes_ref, mean_ref, var_ref)
+    for index, (step, start, many) in enumerate(parts):
+        place = MINE * ids[2 * SLOTS + step] + start
+        for channel in range(many):
+            live = mask[place + channel].astype(jnp.float32)
+            for rows, blended, spread in bands:
+                off = power_ref[index, channel, rows] - blended
+                stage[index, channel, rows] = live / (1.0 + off * off / spread)
+        copies.append(
+            pltpu.make_async_copy(
+                stage.at[index, pl.ds(0, many)],
+                weight_ref.at[0, pl.ds(place, many)],
+                sems.at[index],
+            )
+        )
+        copies[-1].start()
+    for copy in copies:
+        copy.wait()
+
+
+def weigh(parts, cost, ids, mask, ready, powers):
+    whole = pl.BlockSpec(memory_space=pltpu.VMEM)
+    scalars = pl.BlockSpec(memory_space=pltpu.SMEM)
+    count = len(parts)
+    return pl.pallas_call(
+        lambda *refs: weigh_kernel(parts, *refs),
+        in_specs=[scalars] * 2 + [whole] * 5,
+        out_specs=pl.BlockSpec(memory_space=pltpu.HBM),
+        out_shape=jax.ShapeDtypeStruct((1, MINE * SLOTS, BLOCK, BLOCK), jnp.float32),
+        scratch_shapes=[
+            pltpu.VMEM((count, MINE, BLOCK, BLOCK), jnp.float32),
+            pltpu.SemaphoreType.DMA((count,)),
+        ],
+        compiler_params=pltpu.CompilerParams(vmem_limit_bytes=16 << 20),
+        cost_estimate=pl.CostEstimate(flops=cost, bytes_accessed=1 << 20, transcendentals=0),
+        name="weigh",
+    )(ids, mask, *ready, powers)
+
+
+def finish_kernel(parts, ids, mask, count_ref, planes_ref, mean_ref, var_ref, *refs):
+    pieces, (stokes_ref, weight_ref, loaded, stage, sems) = refs[: len(parts)], refs[-5:]
+    loads, copies = [], []
+    for index, (_, _, many) in enumerate(parts):
+        loads.append(
+            pltpu.make_async_copy(pieces[index], loaded.at[index, pl.ds(0, many)], sems.at[index, 0])
+        )
+        loads[-1].start()
+    bands = bands_of(count_ref, planes_ref, mean_ref, var_ref)
     for index, (step, start, many) in enumerate(parts):
         place = MINE * ids[2 * SLOTS + step] + start
         span, held = pl.ds(place, many), pl.ds(0, many)
@@ -195,13 +294,12 @@
     whole = pl.BlockSpec(memory_space=pltpu.VMEM)
     scalars = pl.BlockSpec(memory_space=pltpu.SMEM)
     placed = pl.BlockSpec(memory_space=pltpu.HBM)
-    anywhere = pl.BlockSpec(memory_space=pl.ANY)
     count = len(parts)
     return pl.pallas_call(
         lambda *refs: finish_kernel(parts, *refs),
         in_specs=[scalars] * 2
         + [whole] * 4
-        + [placed if step == 0 else anywhere for step, _, _ in parts]
+        + [placed] * count
         + [placed] * len(outs),
         out_specs=[placed] * 2,
         out_shape=[
@@ -255,8 +353,11 @@
     last = swap(last, TM, SLOTS, 3)
     planes = parts[:, : 2 * rows].reshape(FREQS, 2, rows, BLOCK).transpose(1, 0, 2, 3)
     ready = (parts[:, 2 * rows], planes.reshape(2, BLOCK, BLOCK), running_mean, running_var)
-    outs = finish(PARTS[:4], 1 << 33, ids, channel_mask, ready, pieces, [])
-    return tuple(finish(PARTS[4:], 1 << 20, ids, channel_mask, ready, [last], outs))
+    stokes, powers = place(PARTS[:4], ids, pieces)
+    weights = weigh(PARTS[:4], 1 << 33, ids, channel_mask, ready, powers)
+    return tuple(
+        finish(PARTS[4:], 1 << 20, ids, channel_mask, ready, [last], [stokes, weights])
+    )
 
 
 def solution(mesh):

time: 280 us -> 277 us (0.989)
  waiting for transfers between devices: 221 us -> 218 us
    all_to_all x3, waiting for transfers between devices: 221 us -> 216 us  [exchange(): return lax.all_to_all(value, names, split_axis=0, concat_axis=0, tiled=True)]
    pallas_call x0 -> x2, Pallas kernels: none -> 4.11 us  [the longest x1 2.69 us: place(): pl.pallas_call(lambda *refs: moving_kernel(parts, *refs), in_specs=[pl.Bl...]
    pallas_call x2 -> x1, Pallas kernels: 4.38 us -> 1.46 us  [finish(): pl.pallas_call(lambda *refs: finish_kernel(parts, *refs), in_specs=[scala...]
  transfers between devices with their start and end apart: 7 -> 7, of which waited for: 3 -> 4; matrix products, arithmetic and copies ran while one was open for 1% -> 1% of each run, Pallas kernels for 2% -> 3%
where the time goes in v4:
time: 277 us; the launch traced here: 276 us
  waiting for transfers between devices  218 us (79%)
  starting transfers between devices  32.4 us (12%)
  Pallas kernels  18.1 us (7%)
  local copies, waits for them, and re-layouts  5.84 us (2%)
    all_to_all x3, waiting for transfers between devices, exchange(): return lax.all_to_all(value, names, split_axis=0, concat_axis=0, tiled=True)  216 us
    all_to_all x3, starting transfers between devices, exchange(): return lax.all_to_all(value, names, split_axis=0, concat_axis=0, tiled=True)  28.9 us
    pallas_call x1, Pallas kernels, correlate(): pl.pallas_call(lambda *refs: correlate_kernel(1.0 / math.sqrt(samples), *...  9.59 us
  transfers between devices with their start and end apart: 7, of which 4 were waited for; matrix products, arithmetic and copies ran while one was open for 1% of the time, Pallas kernels for 3%

profile of v4, /device:TPU:1, one launch (start us, length us, event | category | flops | bytes accessed | tf_op | source)
XLA Modules:
  0.0 276.2 jit_solution(2824265343905820765)
XLA Ops:
  0.6 0.0 copy-start.5
  0.6 0.0 copy-start.10
  0.7 0.0 copy-start.9
  0.7 16.7 %all-to-all-start = ((bf16[512,2,16,256]{3,2,1,0:T(8,128)(2,1)}), bf16[512,2,16,256]{3,2,1,0:T(8,128)(2,1)}, u32[]{:S(2)}, u32[]{:S(2)}) async-start(bf16[512,2,16,256]{3,2,1,0:T(8,128)(2,1)} %param.6), calls=%async_computation | async-start | bytes 16777216 | tf_op jit(solution)/shard_map/all_to_all | solution.py:328
  17.3 0.0 copy-done.5
  17.3 0.1 reshape.54
  17.4 0.0 copy-done.10
  17.4 0.2 select_reduce_fusion.2
  17.6 0.1 iota_compare_fusion
  17.7 0.0 copy-done.9
  17.7 0.1 select_reduce_fusion
  17.9 0.1 select_reduce_fusion.1
  17.9 0.6 pad_add_fusion.refs_0_
  18.6 186.1 %all-to-all-done = bf16[512,2,16,256]{3,2,1,0:T(8,128)(2,1)} async-done(((bf16[512,2,16,256]{3,2,1,0:T(8,128)(2,1)}), bf16[512,2,16,256]{3,2,1,0:T(8,128)(2,1)}, u32[]{:S(2)}, u32[]{:S(2)}) %all-to-all-start) | async-done | bytes 8388640 | tf_op jit(solution)/shard_map/all_to_all | solution.py:328
  204.7 0.0 copy-start.7
  204.7 9.6 %correlate.1 = (f32[2,4,2,128,128]{4,3,2,1,0:T(8,128)}, f32[2,4,2,128,128]{4,3,2,1,0:T(8,128)}, f32[2,4,2,128,128]{4,3,2,1,0:T(8,128)}, f32[1,4,2,128,128]{4,3,2...) custom-call(s32[14]{0:T(128)} %pad_add_fusion.refs_0_, ...), custom_call_target="tpu_custom_call" | custom-call | flops 4294967296 | bytes 13631488 | tf_op jit(solution)/shard_map/correlate/pallas_call | solution.py:94
  214.3 0.0 copy-start.3
  214.3 0.0 copy-start.4
  214.3 0.0 copy-start.6
  214.3 0.1 collective-permute-start
  214.4 2.0 copy.22
  216.4 6.8 %all-to-all-start.1 = ((f32[256,4,128]{2,1,0:T(4,128)}), f32[256,4,128]{2,1,0:T(4,128)S(1)}, u32[]{:S(2)}, u32[]{:S(2)}) async-start(f32[256,4,128]{2,1,0:T(4,128)} %bitcast.5), calls=%async_computation.1 | async-start | bytes 1048576 | tf_op jit(solution)/shard_map/all_to_all | solution.py:328
  223.3 2.2 collective-permute-start.2
  225.5 0.0 collective-permute-start.3
  225.5 22.6 %all-to-all-done.1.bands_ref = f32[256,4,128]{2,1,0:T(4,128)S(1)} async-done(((f32[256,4,128]{2,1,0:T(4,128)}), f32[256,4,128]{2,1,0:T(4,128)S(1)}, u32[]{:S(2)}, u32[]{:S(2)}) %all-to-all-start.1) | async-done | bytes 524320 | tf_op jit(solution)/shard_map/all_to_all | solution.py:328
  248.1 0.0 copy-start.8
  248.1 0.0 collective-permute-done._.refs_3_
  248.1 0.0 copy-start
  248.1 0.8 copy-done.8
  248.9 0.3 copy-done
  249.3 3.0 %spread_sums.1 = (f32[1,4,2,128,128]{4,3,2,1,0:T(8,128)}, f32[64,5,128]{2,1,0:T(8,128)}) custom-call(s32[8]{0:T(128)} %refs_1_.3, f32[256,4,128]{2,1,0:T(4,128)} %copy-done.8, f32[2,4,2,128,128]{4,3,2,1,0:T(8,128)} %copy-done, f32[1,4,2,128,128]{4,3,2,1,0:T(8,128)} %get-tuple-element.14.held_ref), custom_call_target="tpu_custom_call" | custom-call | flops 262144 | bytes 1048576 | tf_op jit(solution)/shard_map/spread_sums/pallas_call | solution.py:134
  252.3 5.4 %all-to-all-start.2 = ((f32[64,5,128]{2,1,0:T(8,128)}), f32[64,5,128]{2,1,0:T(8,128)S(1)}, u32[]{:S(2)}, u32[]{:S(2)}) async-start(f32[64,5,128]{2,1,0:T(8,128)} %get-tuple-element.15), calls=%async_computation.2 | async-start | bytes 524288 | tf_op jit(solution)/shard_map/all_to_all | solution.py:328
  257.6 1.2 collective-permute-start.1
  258.9 0.0 collective-permute-done.3.refs_4_
  258.9 0.0 collective-permute-done.2.refs_2_
  258.9 0.0 copy-done.7
  258.9 0.0 copy-start.1
  258.9 1.2 copy-done.1
  260.1 0.0 copy-start.2
  260.1 1.2 copy-done.2
  261.3 2.7 place.1
  264.0 7.0 %all-to-all-done.2 = f32[64,5,128]{2,1,0:T(8,128)S(1)} async-done(((f32[64,5,128]{2,1,0:T(8,128)}), f32[64,5,128]{2,1,0:T(8,128)S(1)}, u32[]{:S(2)}, u32[]{:S(2)}) %all-to-all-start.2) | async-done | bytes 163872 | tf_op jit(solution)/shard_map/all_to_all | solution.py:328
  271.2 0.0 copy-done.3
  271.2 0.0 copy-done.4
  271.2 0.0 copy-done.6
  271.2 1.4 weigh.1.refs_8_
  272.6 2.1 collective-permute-done.1.refs_6_
  274.8 1.5 finish_1.1
  (6 shorter events, 0.1 us)
Async XLA Ops:
  0.6 16.7 %copy-start.5 = (s32[8]{0:T(128)S(1)}, s32[8]{0:T(128)}, u32[]{:S(2)}) copy-start(s32[8]{0:T(128)} %refs_1_.3) | copy-start | bytes 100
  0.6 16.8 %copy-start.10 = (s32[4]{0:T(128)S(1)}, s32[4]{0:T(128)}, u32[]{:S(2)}) copy-start(s32[4]{0:T(128)} %param.8) | copy-start | bytes 52
  0.7 17.1 %copy-start.9 = (s32[4,2]{0,1:T(2,128)S(1)}, s32[4,2]{0,1:T(2,128)}, u32[]{:S(2)}) copy-start(s32[4,2]{0,1:T(2,128)} %param.7) | copy-start | bytes 100
  0.7 204.0 %all-to-all-start = ((bf16[512,2,16,256]{3,2,1,0:T(8,128)(2,1)}), bf16[512,2,16,256]{3,2,1,0:T(8,128)(2,1)}, u32[]{:S(2)}, u32[]{:S(2)}) async-start(bf16[512,2,16,256]{3,2,1,0:T(8,128)(2,1)} %param.6), calls=%async_computation | async-start | bytes 16777216 | tf_op jit(solution)/shard_map/all_to_all | solution.py:328
  204.7 54.2 %copy-start.7 = (s32[14]{0:T(128)S(1)}, s32[14]{0:T(128)}, u32[]{:S(2)}) copy-start(s32[14]{0:T(128)} %pad_add_fusion.refs_0_) | copy-start | bytes 172
  214.3 56.9 %copy-start.3 = (f32[1,128,128]{2,1,0:T(8,128)S(1)}, f32[1,128,128]{2,1,0:T(8,128)}, u32[]{:S(2)}) copy-start(f32[1,128,128]{2,1,0:T(8,128)} %refs_4_.3) | copy-start | bytes 196612
  214.3 56.9 %copy-start.4 = (f32[1,128,128]{2,1,0:T(8,128)S(1)}, f32[1,128,128]{2,1,0:T(8,128)}, u32[]{:S(2)}) copy-start(f32[1,128,128]{2,1,0:T(8,128)} %refs_5_.3) | copy-start | bytes 196612
  214.3 56.9 %copy-start.6 = (s32[8]{0:T(128)S(1)}, s32[8]{0:T(128)}, u32[]{:S(2)}) copy-start(s32[8]{0:T(128)} %refs_1_.3) | copy-start | bytes 100
  214.3 33.8 %collective-permute-start = (f32[2,4,2,128,128]{4,3,2,1,0:T(8,128)}, f32[2,4,2,128,128]{4,3,2,1,0:T(8,128)S(1)}, u32[]{:S(2)}, u32[]{:S(2)}) collective-permute-start(f32[2,4,2,128,128]{4,3,2,1,0:T(8,128)} %get-tuple-element.13), channel_id=1, source_target_pairs={{0,2},{1,3},{2,0},{3,1},{4,6},{5,7},{6,4},{7,5},{8,10},{9,11},{10,... | collective-permute-start | bytes 3145736 | tf_op jit(solution)/shard_map/ppermute | solution.py:324
  216.4 31.7 %all-to-all-start.1 = ((f32[256,4,128]{2,1,0:T(4,128)}), f32[256,4,128]{2,1,0:T(4,128)S(1)}, u32[]{:S(2)}, u32[]{:S(2)}) async-start(f32[256,4,128]{2,1,0:T(4,128)} %bitcast.5), calls=%async_computation.1 | async-start | bytes 1048576 | tf_op jit(solution)/shard_map/all_to_all | solution.py:328
  223.3 35.6 %collective-permute-start.2 = (f32[2,4,2,128,128]{4,3,2,1,0:T(8,128)}, f32[2,4,2,128,128]{4,3,2,1,0:T(8,128)S(1)}, u32[]{:S(2)}, u32[]{:S(2)}) collective-permute-start(f32[2,4,2,128,128]{4,3,2,1,0:T(8,128)} %get-tuple-element.18), channel_id=1, source_target_pairs={{0,1},{1,0},{2,3},{3,2},{4,5},{5,4},{6,7},{7,6},{8,9},{9,8},{10,11... | collective-permute-start | bytes 3145736 | tf_op jit(solution)/shard_map/ppermute | solution.py:324
  225.5 33.4 %collective-permute-start.3 = (f32[1,4,2,128,128]{4,3,2,1,0:T(8,128)}, f32[1,4,2,128,128]{4,3,2,1,0:T(8,128)S(1)}, u32[]{:S(2)}, u32[]{:S(2)}) collective-permute-start(f32[1,4,2,128,128]{4,3,2,1,0:T(8,128)} %get-tuple-element.19), channel_id=1, source_target_pairs={{0,3},{1,2},{2,1},{3,0},{4,7},{5,6},{6,5},{7,4},{8,11},{9,10},{10,... | collective-permute-start | bytes 1572872 | tf_op jit(solution)/shard_map/ppermute | solution.py:324
  248.1 0.8 copy-start.8
  248.1 1.2 copy-start
  252.3 18.8 %all-to-all-start.2 = ((f32[64,5,128]{2,1,0:T(8,128)}), f32[64,5,128]{2,1,0:T(8,128)S(1)}, u32[]{:S(2)}, u32[]{:S(2)}) async-start(f32[64,5,128]{2,1,0:T(8,128)} %get-tuple-element.15), calls=%async_computation.2 | async-start | bytes 524288 | tf_op jit(solution)/shard_map/all_to_all | solution.py:328
  257.6 17.1 %collective-permute-start.1 = (f32[1,4,2,128,128]{4,3,2,1,0:T(8,128)}, f32[1,4,2,128,128]{4,3,2,1,0:T(8,128)S(1)}, u32[]{:S(2)}, u32[]{:S(2)}) collective-permute-start(f32[1,4,2,128,128]{4,3,2,1,0:T(8,128)} %get-tuple-element.16), channel_id=1, source_target_pairs={{0,3},{1,2},{2,1},{3,0},{4,7},{5,6},{6,5},{7,4},{8,11},{9,10},{10,... | collective-permute-start | bytes 1572872 | tf_op jit(solution)/shard_map/ppermute | solution.py:324
  258.9 1.2 copy-start.1
  260.1 1.2 copy-start.2

commit v5 on v4

--- a/solution.py
+++ b/solution.py
@@ -28,39 +28,51 @@
     )
 
 
-def correlate_kernel(scale, ids, turned_ref, *refs):
-    outs, moment_ref = refs[: len(PARTS)], refs[len(PARTS)]
-    loaded, stage, load_sems, sems = refs[len(PARTS) + 1 :]
-    blocks, per_block, pieces, _, _, signals, depth = turned_ref.shape
+def correlate_kernel(scale, steps, ids, turned_ref, *refs):
+    refs = list(refs)
+    early_ref = refs.pop(0) if len(steps) > 1 else None
+    kept = [part for part in PARTS if part[0] in steps]
+    outs, moment_ref = refs[: len(kept)], refs[len(kept)]
+    loaded, stage, load_sems, sems = refs[len(kept) + 1 :]
+    _, per_block, pieces, _, _, signals, depth = turned_ref.shape
     width = per_block * signals
-
-    def load(channel, block):
+    places = loaded.shape[1]
+    low, high = slice(0, BLOCK), slice(BLOCK, 2 * BLOCK)
+
+    def load(channel, place):
+        block = place if early_ref is not None else ids[steps[0] + place * SLOTS]
         return pltpu.make_async_copy(
-            turned_ref.at[block, :, :, channel], loaded.at[channel, block], load_sems.at[channel, block]
-        )
-
-    def copy(number, channel):
-        for out, (step, first, many) in zip(outs, PARTS):
-            if step == number and first <= channel < first + many:
+            turned_ref.at[block, :, :, channel], loaded.at[channel, place], load_sems.at[channel, place]
+        )
+
+    def copy(index, channel):
+        for out, (step, first, many) in zip(outs, kept):
+            if step == steps[index] and first <= channel < first + many:
                 return pltpu.make_async_copy(
-                    stage.at[number, channel], out.at[channel - first], sems.at[number, channel]
+                    stage.at[index, channel], out.at[channel - first], sems.at[index, channel]
                 )
 
-    def side(channel, block, part):
+    def side(channel, place, part):
         return [
-            loaded[channel, block, :, piece, part].reshape(width, depth) for piece in range(pieces)
+            loaded[channel, place, :, piece, part].reshape(width, depth) for piece in range(pieces)
         ]
 
     for channel in range(MINE):
-        for block in range(blocks):
-            load(channel, block).start()
-    low, high = slice(0, BLOCK), slice(BLOCK, 2 * BLOCK)
+        for place in range(places):
+            load(channel, place).start()
+    if early_ref is not None:
+        for step in set(range(SLOTS)) - set(steps):
+            moment_ref[ids[2 * SLOTS + step]] = early_ref[0]
     for channel in range(MINE):
         live = ids[3 * SLOTS + channel].astype(jnp.float32)
-        for block in range(blocks):
-            load(channel, block).wait()
-        for number in range(SLOTS):
-            row, col, slot = ids[number], ids[SLOTS + number], ids[2 * SLOTS + number]
+        for place in range(places):
+            load(channel, place).wait()
+        for index, step in enumerate(steps):
+            row, col, slot = (
+                (0, 1, 0)
+                if early_ref is None
+                else (ids[step], ids[SLOTS + step], ids[2 * SLOTS + step])
+            )
             row_re, row_im = side(channel, row, 0), side(channel, row, 1)
             columns = jnp.concatenate(side(channel, col, 0) + side(channel, col, 1), axis=1)
             real = nt(jnp.concatenate(row_re + row_im, axis=1), columns) * scale
@@ -68,15 +80,15 @@
             imag = nt(jnp.concatenate(row_im + minus_re, axis=1), columns) * scale
             i_re = real[low, low] + real[high, high]
             i_im = imag[low, low] + imag[high, high]
-            stage[number, channel, 0, 0] = i_re
-            stage[number, channel, 0, 1] = i_im
-            stage[number, channel, 1, 0] = real[low, low] - real[high, high]
-            stage[number, channel, 1, 1] = imag[low, low] - imag[high, high]
-            stage[number, channel, 2, 0] = real[low, high] + real[high, low]
-            stage[number, channel, 2, 1] = imag[low, high] + imag[high, low]
-            stage[number, channel, 3, 0] = imag[low, high] - imag[high, low]
-            stage[number, channel, 3, 1] = real[high, low] - real[low, high]
-            copy(number, channel).start()
+            stage[index, channel, 0, 0] = i_re
+            stage[index, channel, 0, 1] = i_im
+            stage[index, channel, 1, 0] = real[low, low] - real[high, high]
+            stage[index, channel, 1, 1] = imag[low, low] - imag[high, high]
+            stage[index, channel, 2, 0] = real[low, high] + real[high, low]
+            stage[index, channel, 2, 1] = imag[low, high] + imag[high, low]
+            stage[index, channel, 3, 0] = imag[low, high] - imag[high, low]
+            stage[index, channel, 3, 1] = real[high, low] - real[low, high]
+            copy(index, channel).start()
             power = i_re * i_re + i_im * i_im
             masked = power * live
             for order, plane in enumerate((masked, masked * power)):
@@ -84,33 +96,37 @@
                     plane = plane + moment_ref[slot, order]
                 moment_ref[slot, order] = plane
     for channel in range(MINE):
-        for number in range(SLOTS):
-            copy(number, channel).wait()
-
-
-def correlate(ids, turned, samples):
+        for index in range(len(steps)):
+            copy(index, channel).wait()
+
+
+def correlate(steps, ids, turned, early, samples):
     blocks, per_block, pieces, channels, _, signals, depth = turned.shape
+    kept = [part for part in PARTS if part[0] in steps]
+    many = len(steps)
+    places, slots = (blocks, SLOTS) if many > 1 else (2, 1)
     anywhere = pl.BlockSpec(memory_space=pl.ANY)
-    return pl.pallas_call(
-        lambda *refs: correlate_kernel(1.0 / math.sqrt(samples), *refs),
-        in_specs=[pl.BlockSpec(memory_space=pltpu.SMEM), anywhere],
-        out_specs=[anywhere] * len(PARTS) + [pl.BlockSpec(memory_space=pltpu.VMEM)],
+    whole = pl.BlockSpec(memory_space=pltpu.VMEM)
+    return pl.pallas_call(
+        lambda *refs: correlate_kernel(1.0 / math.sqrt(samples), steps, *refs),
+        in_specs=[pl.BlockSpec(memory_space=pltpu.SMEM), anywhere] + [whole] * len(early),
+        out_specs=[anywhere] * len(kept) + [whole],
         scratch_shapes=[
-            pltpu.VMEM((channels, blocks, per_block, pieces, 2, signals, depth), turned.dtype),
-            pltpu.VMEM((SLOTS, channels) + PLANES, jnp.float32),
-            pltpu.SemaphoreType.DMA((channels, blocks)),
-            pltpu.SemaphoreType.DMA((SLOTS, channels)),
-        ],
-        out_shape=[jax.ShapeDtypeStruct((many,) + PLANES, jnp.float32) for _, _, many in PARTS]
-        + [jax.ShapeDtypeStruct((SLOTS, 2, BLOCK, BLOCK), jnp.float32)],
+            pltpu.VMEM((channels, places, per_block, pieces, 2, signals, depth), turned.dtype),
+            pltpu.VMEM((many, channels) + PLANES, jnp.float32),
+            pltpu.SemaphoreType.DMA((channels, places)),
+            pltpu.SemaphoreType.DMA((many, channels)),
+        ],
+        out_shape=[jax.ShapeDtypeStruct((count,) + PLANES, jnp.float32) for _, _, count in kept]
+        + [jax.ShapeDtypeStruct((slots, 2, BLOCK, BLOCK), jnp.float32)],
         compiler_params=pltpu.CompilerParams(vmem_limit_bytes=56 << 20),
         cost_estimate=pl.CostEstimate(
-            flops=SLOTS * channels * 8 * (2 * BLOCK) ** 2 * samples,
-            bytes_accessed=13 << 20,
+            flops=many * channels * 8 * (2 * BLOCK) ** 2 * samples,
+            bytes_accessed=(places + many) * channels << 20,
             transcendentals=0,
         ),
-        name="correlate",
-    )(ids, turned)
+        name=f"correlate_{many}",
+    )(ids, turned, *early)
 
 
 def spread_kernel(mask, bands_ref, _, held_ref, passed_ref, part_ref, sem):
@@ -342,7 +358,9 @@
 
     turned = exchange(voltages, ALL)
     turned = turned.reshape(4, FREQS // 4, SLOTS, MINE, 2, signals, depth)
-    *held, moments = correlate(ids, turned, depth * SLOTS)
+    crossing, early = correlate((2,), ids, turned, [], depth * SLOTS)
+    *held, moments = correlate((0, 1, 3), ids, turned, [early], depth * SLOTS)
+    held.insert(2, crossing)
     pieces = held[:1] + [swap(held[number], TM, SLOTS, number) for number in range(1, SLOTS)]
 
     rows = BLOCK // FREQS

time: 277 us -> 276 us (level)
  Pallas kernels: 18.1 us -> 22.5 us
  waiting for transfers between devices: 218 us -> 214 us
    pallas_call x1 -> x2, Pallas kernels: 9.59 us -> 13.9 us  [correlate(): pl.pallas_call(lambda *refs: correlate_kernel(1.0 / math.sqrt(samples), s...]
    all_to_all x3, waiting for transfers between devices: 216 us -> 211 us  [exchange(): return lax.all_to_all(value, names, split_axis=0, concat_axis=0, tiled=True)]
  transfers between devices with their start and end apart: 7 -> 7, of which waited for: 4 -> 4; matrix products, arithmetic and copies ran while one was open for 1% -> 1% of each run, Pallas kernels for 3% -> 6%
where the time goes in v5:
time: 276 us
  waiting for transfers between devices  214 us (78%)
  starting transfers between devices  31.9 us (12%)
  Pallas kernels  22.5 us (8%)
  local copies, waits for them, and re-layouts  5.82 us (2%)
    all_to_all x3, waiting for transfers between devices, exchange(): return lax.all_to_all(value, names, split_axis=0, concat_axis=0, tiled=True)  211 us
    all_to_all x3, starting transfers between devices, exchange(): return lax.all_to_all(value, names, split_axis=0, concat_axis=0, tiled=True)  28.1 us
    pallas_call x2, Pallas kernels, correlate(): pl.pallas_call(lambda *refs: correlate_kernel(1.0 / math.sqrt(samples), s...  13.9 us
  transfers between devices with their start and end apart: 7, of which 4 were waited for; matrix products, arithmetic and copies ran while one was open for 1% of the time, Pallas kernels for 6%

profile of v5, /device:TPU:1, one launch (start us, length us, event | category | flops | bytes accessed | tf_op | source)
XLA Modules:
  0.0 275.7 jit_solution(8516508125283016892)
XLA Ops:
  0.6 0.0 copy-start.6
  0.6 0.0 copy-start.10
  0.7 0.0 copy-start.9
  0.7 16.7 %all-to-all-start = ((bf16[512,2,16,256]{3,2,1,0:T(8,128)(2,1)}), bf16[512,2,16,256]{3,2,1,0:T(8,128)(2,1)}, u32[]{:S(2)}, u32[]{:S(2)}) async-start(bf16[512,2,16,256]{3,2,1,0:T(8,128)(2,1)} %param.6), calls=%async_computation | async-start | bytes 16777216 | tf_op jit(solution)/shard_map/all_to_all | solution.py:344
  17.3 0.0 copy-done.6
  17.3 0.1 reshape.54
  17.4 0.0 copy-done.10
  17.4 0.2 select_reduce_fusion.2
  17.6 0.1 iota_compare_fusion
  17.7 0.0 copy-done.9
  17.7 0.1 select_reduce_fusion
  17.9 0.1 select_reduce_fusion.1
  17.9 0.6 pad_add_fusion.refs_0_
  18.6 186.1 %all-to-all-done = bf16[512,2,16,256]{3,2,1,0:T(8,128)(2,1)} async-done(((bf16[512,2,16,256]{3,2,1,0:T(8,128)(2,1)}), bf16[512,2,16,256]{3,2,1,0:T(8,128)(2,1)}, u32[]{:S(2)}, u32[]{:S(2)}) %all-to-all-start) | async-done | bytes 8388640 | tf_op jit(solution)/shard_map/all_to_all | solution.py:344
  204.7 5.3 %correlate_1.1 = (f32[2,4,2,128,128]{4,3,2,1,0:T(8,128)}, f32[1,2,128,128]{3,2,1,0:T(8,128)}) custom-call(s32[14]{0:T(128)} %pad_add_fusion.refs_0_, bf16[4,16,4,2,2,16,256]{6,5,4,3,2,1,0:T(8,128)(2,1)} %bitcast.2.refs_1_), custom_call_target="tpu_custom_call" | custom-call | flops 1073741824 | bytes 6291456 | tf_op jit(solution)/shard_map/correlate_1/pallas_call | solution.py:110
  209.9 0.0 copy-start.5
  210.0 0.1 collective-permute-start
  210.1 0.0 copy-start.3
  210.1 0.0 copy-start.4
  210.1 0.0 copy-start.7
  210.1 8.6 %correlate_3.1 = (f32[2,4,2,128,128]{4,3,2,1,0:T(8,128)}, f32[2,4,2,128,128]{4,3,2,1,0:T(8,128)}, f32[1,4,2,128,128]{4,3,2,1,0:T(8,128)}, f32[1,4,2,128,128]{4,3,2,1,0:T(8,128)}, f32[4,2,128,128]{3,2,1,0:T(8,128)}) custom-call(s32[14]{0:T(128)} %pad_add_fusion.refs_0_, bf16[4,16,4,2,2,16,256]{6,5,4,3,2,1,0:T(8,128)(2,1)} %bitcast.2.refs_1_, ...), custom_call_target="tpu_custom_call" | custom-call | flops 3221225472 | bytes 14680064 | tf_op jit(solution)/shard_map/correlate_3/pallas_call | solution.py:110
  218.7 2.0 copy.22
  220.7 6.8 %all-to-all-start.1 = ((f32[256,4,128]{2,1,0:T(4,128)}), f32[256,4,128]{2,1,0:T(4,128)S(1)}, u32[]{:S(2)}, u32[]{:S(2)}) async-start(f32[256,4,128]{2,1,0:T(4,128)} %bitcast.5), calls=%async_computation.1 | async-start | bytes 1048576 | tf_op jit(solution)/shard_map/all_to_all | solution.py:344
  227.5 2.2 collective-permute-start.2
  229.8 0.0 collective-permute-start.3
  229.8 18.8 %all-to-all-done.1.bands_ref = f32[256,4,128]{2,1,0:T(4,128)S(1)} async-done(((f32[256,4,128]{2,1,0:T(4,128)}), f32[256,4,128]{2,1,0:T(4,128)S(1)}, u32[]{:S(2)}, u32[]{:S(2)}) %all-to-all-start.1) | async-done | bytes 524320 | tf_op jit(solution)/shard_map/all_to_all | solution.py:344
  248.6 0.0 copy-start.8
  248.6 0.0 collective-permute-done._.refs_3_
  248.6 0.0 copy-start
  248.6 0.8 copy-done.8
  249.4 0.3 copy-done
  249.7 3.0 %spread_sums.1 = (f32[1,4,2,128,128]{4,3,2,1,0:T(8,128)}, f32[64,5,128]{2,1,0:T(8,128)}) custom-call(s32[8]{0:T(128)} %refs_1_.3, f32[256,4,128]{2,1,0:T(4,128)} %copy-done.8, f32[2,4,2,128,128]{4,3,2,1,0:T(8,128)} %copy-done, f32[1,4,2,128,128]{4,3,2,1,0:T(8,128)} %get-tuple-element.16.held_ref), custom_call_target="tpu_custom_call" | custom-call | flops 262144 | bytes 1048576 | tf_op jit(solution)/shard_map/spread_sums/pallas_call | solution.py:150
  252.8 4.6 %all-to-all-start.2 = ((f32[64,5,128]{2,1,0:T(8,128)}), f32[64,5,128]{2,1,0:T(8,128)S(1)}, u32[]{:S(2)}, u32[]{:S(2)}) async-start(f32[64,5,128]{2,1,0:T(8,128)} %get-tuple-element.17), calls=%async_computation.2 | async-start | bytes 524288 | tf_op jit(solution)/shard_map/all_to_all | solution.py:344
  257.4 1.5 collective-permute-start.1
  258.9 0.0 collective-permute-done.3.refs_4_
  258.9 0.0 collective-permute-done.2.refs_2_
  258.9 0.0 copy-done.5
  258.9 0.0 copy-start.1
  258.9 1.2 copy-done.1
  260.1 1.2 copy-done.2
  261.3 2.7 place.1
  264.0 6.5 %all-to-all-done.2 = f32[64,5,128]{2,1,0:T(8,128)S(1)} async-done(((f32[64,5,128]{2,1,0:T(8,128)}), f32[64,5,128]{2,1,0:T(8,128)S(1)}, u32[]{:S(2)}, u32[]{:S(2)}) %all-to-all-start.2) | async-done | bytes 163872 | tf_op jit(solution)/shard_map/all_to_all | solution.py:344
  270.6 0.0 copy-done.3
  270.6 0.0 copy-done.4
  270.6 0.0 copy-done.7
  270.7 1.4 weigh.1.refs_8_
  272.1 2.2 collective-permute-done.1.refs_6_
  274.2 1.5 finish_1.1
  (7 shorter events, 0.1 us)
Async XLA Ops:
  0.6 16.7 %copy-start.6 = (s32[8]{0:T(128)S(1)}, s32[8]{0:T(128)}, u32[]{:S(2)}) copy-start(s32[8]{0:T(128)} %refs_1_.3) | copy-start | bytes 100
  0.6 16.8 %copy-start.10 = (s32[4]{0:T(128)S(1)}, s32[4]{0:T(128)}, u32[]{:S(2)}) copy-start(s32[4]{0:T(128)} %param.8) | copy-start | bytes 52
  0.7 17.1 %copy-start.9 = (s32[4,2]{0,1:T(2,128)S(1)}, s32[4,2]{0,1:T(2,128)}, u32[]{:S(2)}) copy-start(s32[4,2]{0,1:T(2,128)} %param.7) | copy-start | bytes 100
  0.7 204.0 %all-to-all-start = ((bf16[512,2,16,256]{3,2,1,0:T(8,128)(2,1)}), bf16[512,2,16,256]{3,2,1,0:T(8,128)(2,1)}, u32[]{:S(2)}, u32[]{:S(2)}) async-start(bf16[512,2,16,256]{3,2,1,0:T(8,128)(2,1)} %param.6), calls=%async_computation | async-start | bytes 16777216 | tf_op jit(solution)/shard_map/all_to_all | solution.py:344
  209.9 48.9 %copy-start.5 = (s32[14]{0:T(128)S(1)}, s32[14]{0:T(128)}, u32[]{:S(2)}) copy-start(s32[14]{0:T(128)} %pad_add_fusion.refs_0_) | copy-start | bytes 172
  210.0 38.6 %collective-permute-start = (f32[2,4,2,128,128]{4,3,2,1,0:T(8,128)}, f32[2,4,2,128,128]{4,3,2,1,0:T(8,128)S(1)}, u32[]{:S(2)}, u32[]{:S(2)}) collective-permute-start(f32[2,4,2,128,128]{4,3,2,1,0:T(8,128)} %get-tuple-element.15), channel_id=1, source_target_pairs={{0,2},{1,3},{2,0},{3,1},{4,6},{5,7},{6,4},{7,5},{8,10},{9,11},{10,... | collective-permute-start | bytes 3145736 | tf_op jit(solution)/shard_map/ppermute | solution.py:340
  210.1 60.6 %copy-start.3 = (f32[1,128,128]{2,1,0:T(8,128)S(1)}, f32[1,128,128]{2,1,0:T(8,128)}, u32[]{:S(2)}) copy-start(f32[1,128,128]{2,1,0:T(8,128)} %refs_4_.3) | copy-start | bytes 196612
  210.1 60.6 %copy-start.4 = (f32[1,128,128]{2,1,0:T(8,128)S(1)}, f32[1,128,128]{2,1,0:T(8,128)}, u32[]{:S(2)}) copy-start(f32[1,128,128]{2,1,0:T(8,128)} %refs_5_.3) | copy-start | bytes 196612
  210.1 60.6 %copy-start.7 = (s32[8]{0:T(128)S(1)}, s32[8]{0:T(128)}, u32[]{:S(2)}) copy-start(s32[8]{0:T(128)} %refs_1_.3) | copy-start | bytes 100
  220.7 27.9 %all-to-all-start.1 = ((f32[256,4,128]{2,1,0:T(4,128)}), f32[256,4,128]{2,1,0:T(4,128)S(1)}, u32[]{:S(2)}, u32[]{:S(2)}) async-start(f32[256,4,128]{2,1,0:T(4,128)} %bitcast.5), calls=%async_computation.1 | async-start | bytes 1048576 | tf_op jit(solution)/shard_map/all_to_all | solution.py:344
  227.5 31.4 %collective-permute-start.2 = (f32[2,4,2,128,128]{4,3,2,1,0:T(8,128)}, f32[2,4,2,128,128]{4,3,2,1,0:T(8,128)S(1)}, u32[]{:S(2)}, u32[]{:S(2)}) collective-permute-start(f32[2,4,2,128,128]{4,3,2,1,0:T(8,128)} %get-tuple-element.20), channel_id=1, source_target_pairs={{0,1},{1,0},{2,3},{3,2},{4,5},{5,4},{6,7},{7,6},{8,9},{9,8},{10,11... | collective-permute-start | bytes 3145736 | tf_op jit(solution)/shard_map/ppermute | solution.py:340
  229.8 29.1 %collective-permute-start.3 = (f32[1,4,2,128,128]{4,3,2,1,0:T(8,128)}, f32[1,4,2,128,128]{4,3,2,1,0:T(8,128)S(1)}, u32[]{:S(2)}, u32[]{:S(2)}) collective-permute-start(f32[1,4,2,128,128]{4,3,2,1,0:T(8,128)} %get-tuple-element.21), channel_id=1, source_target_pairs={{0,3},{1,2},{2,1},{3,0},{4,7},{5,6},{6,5},{7,4},{8,11},{9,10},{10,... | collective-permute-start | bytes 1572872 | tf_op jit(solution)/shard_map/ppermute | solution.py:340
  248.6 0.8 copy-start.8
  248.6 1.1 copy-start
  252.8 17.7 %all-to-all-start.2 = ((f32[64,5,128]{2,1,0:T(8,128)}), f32[64,5,128]{2,1,0:T(8,128)S(1)}, u32[]{:S(2)}, u32[]{:S(2)}) async-start(f32[64,5,128]{2,1,0:T(8,128)} %get-tuple-element.17), calls=%async_computation.2 | async-start | bytes 524288 | tf_op jit(solution)/shard_map/all_to_all | solution.py:344
  257.4 16.9 %collective-permute-start.1 = (f32[1,4,2,128,128]{4,3,2,1,0:T(8,128)}, f32[1,4,2,128,128]{4,3,2,1,0:T(8,128)S(1)}, u32[]{:S(2)}, u32[]{:S(2)}) collective-permute-start(f32[1,4,2,128,128]{4,3,2,1,0:T(8,128)} %get-tuple-element.18), channel_id=1, source_target_pairs={{0,3},{1,2},{2,1},{3,0},{4,7},{5,6},{6,5},{7,4},{8,11},{9,10},{10,... | collective-permute-start | bytes 1572872 | tf_op jit(solution)/shard_map/ppermute | solution.py:340
  258.9 1.2 copy-start.1
  260.1 1.2 copy-start.2

commit v6 on v5

--- a/solution.py
+++ b/solution.py
@@ -32,8 +32,9 @@
     refs = list(refs)
     early_ref = refs.pop(0) if len(steps) > 1 else None
     kept = [part for part in PARTS if part[0] in steps]
-    outs, moment_ref = refs[: len(kept)], refs[len(kept)]
-    loaded, stage, load_sems, sems = refs[len(kept) + 1 :]
+    outs, sum_ref = refs[: len(kept)], refs[len(kept)]
+    loaded, stage, load_sems, sems = refs[len(kept) + 1 : len(kept) + 5]
+    moment_ref = sum_ref if early_ref is None else refs[-1]
     _, per_block, pieces, _, _, signals, depth = turned_ref.shape
     width = per_block * signals
     places = loaded.shape[1]
@@ -95,6 +96,13 @@
                 if channel > 0:
                     plane = plane + moment_ref[slot, order]
                 moment_ref[slot, order] = plane
+    if early_ref is not None:
+        rows = BLOCK // FREQS
+        for slot in range(SLOTS):
+            for order in range(2):
+                sum_ref[:, slot, pl.ds(order * rows, rows)] = moment_ref[slot, order].reshape(
+                    FREQS, rows, BLOCK
+                )
     for channel in range(MINE):
         for index in range(len(steps)):
             copy(index, channel).wait()
@@ -104,7 +112,8 @@
     blocks, per_block, pieces, channels, _, signals, depth = turned.shape
     kept = [part for part in PARTS if part[0] in steps]
     many = len(steps)
-    places, slots = (blocks, SLOTS) if many > 1 else (2, 1)
+    places = blocks if many > 1 else 2
+    sums = (FREQS, SLOTS, 2 * BLOCK // FREQS, BLOCK) if many > 1 else (1, 2, BLOCK, BLOCK)
     anywhere = pl.BlockSpec(memory_space=pl.ANY)
     whole = pl.BlockSpec(memory_space=pltpu.VMEM)
     return pl.pallas_call(
@@ -116,9 +125,10 @@
             pltpu.VMEM((many, channels) + PLANES, jnp.float32),
             pltpu.SemaphoreType.DMA((channels, places)),
             pltpu.SemaphoreType.DMA((many, channels)),
-        ],
+        ]
+        + [pltpu.VMEM((SLOTS, 2, BLOCK, BLOCK), jnp.float32)] * len(early),
         out_shape=[jax.ShapeDtypeStruct((count,) + PLANES, jnp.float32) for _, _, count in kept]
-        + [jax.ShapeDtypeStruct((slots, 2, BLOCK, BLOCK), jnp.float32)],
+        + [jax.ShapeDtypeStruct(sums, jnp.float32)],
         compiler_params=pltpu.CompilerParams(vmem_limit_bytes=56 << 20),
         cost_estimate=pl.CostEstimate(
             flops=many * channels * 8 * (2 * BLOCK) ** 2 * samples,
@@ -364,8 +374,7 @@
     pieces = held[:1] + [swap(held[number], TM, SLOTS, number) for number in range(1, SLOTS)]
 
     rows = BLOCK // FREQS
-    part = moments.reshape(SLOTS, 2, FREQS, rows, BLOCK).transpose(2, 0, 1, 3, 4)
-    part = exchange(part.reshape(FREQS * SLOTS, 2 * rows, BLOCK), ALL)
+    part = exchange(moments.reshape(FREQS * SLOTS, 2 * rows, BLOCK), ALL)
     last, part = spread_sums(channel_mask, part, pieces[2], held[4])
     parts = exchange(part, FREQ)
     last = swap(last, TM, SLOTS, 3)

time: 276 us -> 274 us (level)
  transfers between devices with their start and end apart: 7 -> 7, of which waited for: 4 -> 4; matrix products, arithmetic and copies ran while one was open for 1% -> 0% of each run, Pallas kernels for 6% -> 6%
where the time goes in v6:
time: 274 us
  waiting for transfers between devices  214 us (78%)
  starting transfers between devices  31.8 us (12%)
  Pallas kernels  22.4 us (8%)
  local copies, waits for them, and re-layouts  3.81 us (1%)
    all_to_all x3, waiting for transfers between devices, exchange(): return lax.all_to_all(value, names, split_axis=0, concat_axis=0, tiled=True)  212 us
    all_to_all x3, starting transfers between devices, exchange(): return lax.all_to_all(value, names, split_axis=0, concat_axis=0, tiled=True)  28.1 us
    pallas_call x2, Pallas kernels, correlate(): pl.pallas_call(lambda *refs: correlate_kernel(1.0 / math.sqrt(samples), s...  13.9 us
  transfers between devices with their start and end apart: 7, of which 4 were waited for; matrix products, arithmetic and copies ran while one was open for 0% of the time, Pallas kernels for 6%

profile of v6, /device:TPU:1, one launch (start us, length us, event | category | flops | bytes accessed | tf_op | source)
XLA Modules:
  0.0 273.8 jit_solution(6723039378766248313)
XLA Ops:
  0.6 0.0 copy-start.6
  0.6 0.0 copy-start.10
  0.7 0.0 copy-start.9
  0.7 16.7 %all-to-all-start = ((bf16[512,2,16,256]{3,2,1,0:T(8,128)(2,1)}), bf16[512,2,16,256]{3,2,1,0:T(8,128)(2,1)}, u32[]{:S(2)}, u32[]{:S(2)}) async-start(bf16[512,2,16,256]{3,2,1,0:T(8,128)(2,1)} %param.6), calls=%async_computation | async-start | bytes 16777216 | tf_op jit(solution)/shard_map/all_to_all | solution.py:354
  17.3 0.0 copy-done.6
  17.3 0.1 reshape.51
  17.4 0.0 copy-done.10
  17.4 0.2 select_reduce_fusion.2
  17.6 0.1 iota_compare_fusion
  17.7 0.0 copy-done.9
  17.7 0.1 select_reduce_fusion
  17.9 0.1 select_reduce_fusion.1
  17.9 0.6 pad_add_fusion.refs_0_
  18.6 186.1 %all-to-all-done = bf16[512,2,16,256]{3,2,1,0:T(8,128)(2,1)} async-done(((bf16[512,2,16,256]{3,2,1,0:T(8,128)(2,1)}), bf16[512,2,16,256]{3,2,1,0:T(8,128)(2,1)}, u32[]{:S(2)}, u32[]{:S(2)}) %all-to-all-start) | async-done | bytes 8388640 | tf_op jit(solution)/shard_map/all_to_all | solution.py:354
  204.7 5.2 %correlate_1.1 = (f32[2,4,2,128,128]{4,3,2,1,0:T(8,128)}, f32[1,2,128,128]{3,2,1,0:T(8,128)}) custom-call(s32[14]{0:T(128)} %pad_add_fusion.refs_0_, bf16[4,16,4,2,2,16,256]{6,5,4,3,2,1,0:T(8,128)(2,1)} %bitcast.2.refs_1_), custom_call_target="tpu_custom_call" | custom-call | flops 1073741824 | bytes 6291456 | tf_op jit(solution)/shard_map/correlate_1/pallas_call | solution.py:119
  209.9 0.0 copy-start.5
  209.9 0.1 collective-permute-start
  210.0 0.0 copy-start.3
  210.0 0.0 copy-start.4
  210.0 0.0 copy-start.7
  210.1 8.6 %correlate_3.1 = (f32[2,4,2,128,128]{4,3,2,1,0:T(8,128)}, f32[2,4,2,128,128]{4,3,2,1,0:T(8,128)}, f32[1,4,2,128,128]{4,3,2,1,0:T(8,128)}, f32[1,4,2,128,128]{4,3,2,1,0:T(8,128)}, f32[64,4,4,128]{3,2,1,0:T(4,128)}) custom-call(s32[14]{0:T(128)} %pad_add_fusion.refs_0_, bf16[4,16,4,2,2,16,256]{6,5,4,3,2,1,0:T(8,128)(2,1)} %bitcast.2.refs_1_, ...), custom_call_target="tpu_custom_call" | custom-call | flops 3221225472 | bytes 14680064 | tf_op jit(solution)/shard_map/correlate_3/pallas_call | solution.py:119
  218.7 6.8 %all-to-all-start.1 = ((f32[256,4,128]{2,1,0:T(4,128)}), f32[256,4,128]{2,1,0:T(4,128)S(1)}, u32[]{:S(2)}, u32[]{:S(2)}) async-start(f32[256,4,128]{2,1,0:T(4,128)} %bitcast.17), calls=%async_computation.1 | async-start | bytes 1048576 | tf_op jit(solution)/shard_map/all_to_all | solution.py:354
  225.5 2.2 collective-permute-start.2
  227.8 0.0 collective-permute-start.3
  227.8 18.9 %all-to-all-done.1.bands_ref = f32[256,4,128]{2,1,0:T(4,128)S(1)} async-done(((f32[256,4,128]{2,1,0:T(4,128)}), f32[256,4,128]{2,1,0:T(4,128)S(1)}, u32[]{:S(2)}, u32[]{:S(2)}) %all-to-all-start.1) | async-done | bytes 524320 | tf_op jit(solution)/shard_map/all_to_all | solution.py:354
  246.7 0.0 copy-start.8
  246.7 0.0 collective-permute-done._.refs_3_
  246.7 0.0 copy-start
  246.7 0.8 copy-done.8
  247.5 0.3 copy-done
  247.8 3.0 %spread_sums.1 = (f32[1,4,2,128,128]{4,3,2,1,0:T(8,128)}, f32[64,5,128]{2,1,0:T(8,128)}) custom-call(s32[8]{0:T(128)} %refs_1_.3, f32[256,4,128]{2,1,0:T(4,128)} %copy-done.8, f32[2,4,2,128,128]{4,3,2,1,0:T(8,128)} %copy-done, f32[1,4,2,128,128]{4,3,2,1,0:T(8,128)} %get-tuple-element.16.held_ref), custom_call_target="tpu_custom_call" | custom-call | flops 262144 | bytes 1048576 | tf_op jit(solution)/shard_map/spread_sums/pallas_call | solution.py:160
  250.8 4.6 %all-to-all-start.2 = ((f32[64,5,128]{2,1,0:T(8,128)}), f32[64,5,128]{2,1,0:T(8,128)S(1)}, u32[]{:S(2)}, u32[]{:S(2)}) async-start(f32[64,5,128]{2,1,0:T(8,128)} %get-tuple-element.17), calls=%async_computation.2 | async-start | bytes 524288 | tf_op jit(solution)/shard_map/all_to_all | solution.py:354
  255.5 1.4 collective-permute-start.1
  256.9 0.0 collective-permute-done.3.refs_4_
  256.9 0.0 collective-permute-done.2.refs_2_
  256.9 0.0 copy-done.5
  256.9 0.0 copy-start.1
  256.9 1.2 copy-done.1
  258.1 0.0 copy-start.2
  258.1 1.2 copy-done.2
  259.3 2.7 place.1
  262.0 6.7 %all-to-all-done.2 = f32[64,5,128]{2,1,0:T(8,128)S(1)} async-done(((f32[64,5,128]{2,1,0:T(8,128)}), f32[64,5,128]{2,1,0:T(8,128)S(1)}, u32[]{:S(2)}, u32[]{:S(2)}) %all-to-all-start.2) | async-done | bytes 163872 | tf_op jit(solution)/shard_map/all_to_all | solution.py:354
  268.9 0.0 copy-done.3
  268.9 0.0 copy-done.4
  268.9 0.0 copy-done.7
  268.9 1.4 weigh.1.refs_8_
  270.3 2.0 collective-permute-done.1.refs_6_
  272.3 1.5 finish_1.1
  (6 shorter events, 0.1 us)
Async XLA Ops:
  0.6 16.7 %copy-start.6 = (s32[8]{0:T(128)S(1)}, s32[8]{0:T(128)}, u32[]{:S(2)}) copy-start(s32[8]{0:T(128)} %refs_1_.3) | copy-start | bytes 100
  0.6 16.8 %copy-start.10 = (s32[4]{0:T(128)S(1)}, s32[4]{0:T(128)}, u32[]{:S(2)}) copy-start(s32[4]{0:T(128)} %param.8) | copy-start | bytes 52
  0.7 17.1 %copy-start.9 = (s32[4,2]{0,1:T(2,128)S(1)}, s32[4,2]{0,1:T(2,128)}, u32[]{:S(2)}) copy-start(s32[4,2]{0,1:T(2,128)} %param.7) | copy-start | bytes 100
  0.7 204.0 %all-to-all-start = ((bf16[512,2,16,256]{3,2,1,0:T(8,128)(2,1)}), bf16[512,2,16,256]{3,2,1,0:T(8,128)(2,1)}, u32[]{:S(2)}, u32[]{:S(2)}) async-start(bf16[512,2,16,256]{3,2,1,0:T(8,128)(2,1)} %param.6), calls=%async_computation | async-start | bytes 16777216 | tf_op jit(solution)/shard_map/all_to_all | solution.py:354
  209.9 47.0 %copy-start.5 = (s32[14]{0:T(128)S(1)}, s32[14]{0:T(128)}, u32[]{:S(2)}) copy-start(s32[14]{0:T(128)} %pad_add_fusion.refs_0_) | copy-start | bytes 172
  209.9 36.8 %collective-permute-start = (f32[2,4,2,128,128]{4,3,2,1,0:T(8,128)}, f32[2,4,2,128,128]{4,3,2,1,0:T(8,128)S(1)}, u32[]{:S(2)}, u32[]{:S(2)}) collective-permute-start(f32[2,4,2,128,128]{4,3,2,1,0:T(8,128)} %get-tuple-element.15), channel_id=1, source_target_pairs={{0,2},{1,3},{2,0},{3,1},{4,6},{5,7},{6,4},{7,5},{8,10},{9,11},{10,... | collective-permute-start | bytes 3145736 | tf_op jit(solution)/shard_map/ppermute | solution.py:350
  210.0 58.8 %copy-start.3 = (f32[1,128,128]{2,1,0:T(8,128)S(1)}, f32[1,128,128]{2,1,0:T(8,128)}, u32[]{:S(2)}) copy-start(f32[1,128,128]{2,1,0:T(8,128)} %refs_4_.3) | copy-start | bytes 196612
  210.0 58.8 %copy-start.4 = (f32[1,128,128]{2,1,0:T(8,128)S(1)}, f32[1,128,128]{2,1,0:T(8,128)}, u32[]{:S(2)}) copy-start(f32[1,128,128]{2,1,0:T(8,128)} %refs_5_.3) | copy-start | bytes 196612
  210.0 58.8 %copy-start.7 = (s32[8]{0:T(128)S(1)}, s32[8]{0:T(128)}, u32[]{:S(2)}) copy-start(s32[8]{0:T(128)} %refs_1_.3) | copy-start | bytes 100
  218.7 28.0 %all-to-all-start.1 = ((f32[256,4,128]{2,1,0:T(4,128)}), f32[256,4,128]{2,1,0:T(4,128)S(1)}, u32[]{:S(2)}, u32[]{:S(2)}) async-start(f32[256,4,128]{2,1,0:T(4,128)} %bitcast.17), calls=%async_computation.1 | async-start | bytes 1048576 | tf_op jit(solution)/shard_map/all_to_all | solution.py:354
  225.5 31.3 %collective-permute-start.2 = (f32[2,4,2,128,128]{4,3,2,1,0:T(8,128)}, f32[2,4,2,128,128]{4,3,2,1,0:T(8,128)S(1)}, u32[]{:S(2)}, u32[]{:S(2)}) collective-permute-start(f32[2,4,2,128,128]{4,3,2,1,0:T(8,128)} %get-tuple-element.20), channel_id=1, source_target_pairs={{0,1},{1,0},{2,3},{3,2},{4,5},{5,4},{6,7},{7,6},{8,9},{9,8},{10,11... | collective-permute-start | bytes 3145736 | tf_op jit(solution)/shard_map/ppermute | solution.py:350
  227.8 29.1 %collective-permute-start.3 = (f32[1,4,2,128,128]{4,3,2,1,0:T(8,128)}, f32[1,4,2,128,128]{4,3,2,1,0:T(8,128)S(1)}, u32[]{:S(2)}, u32[]{:S(2)}) collective-permute-start(f32[1,4,2,128,128]{4,3,2,1,0:T(8,128)} %get-tuple-element.21), channel_id=1, source_target_pairs={{0,3},{1,2},{2,1},{3,0},{4,7},{5,6},{6,5},{7,4},{8,11},{9,10},{10,... | collective-permute-start | bytes 1572872 | tf_op jit(solution)/shard_map/ppermute | solution.py:350
  246.7 0.8 copy-start.8
  246.7 1.1 copy-start
  250.8 17.9 %all-to-all-start.2 = ((f32[64,5,128]{2,1,0:T(8,128)}), f32[64,5,128]{2,1,0:T(8,128)S(1)}, u32[]{:S(2)}, u32[]{:S(2)}) async-start(f32[64,5,128]{2,1,0:T(8,128)} %get-tuple-element.17), calls=%async_computation.2 | async-start | bytes 524288 | tf_op jit(solution)/shard_map/all_to_all | solution.py:354
  255.5 16.8 %collective-permute-start.1 = (f32[1,4,2,128,128]{4,3,2,1,0:T(8,128)}, f32[1,4,2,128,128]{4,3,2,1,0:T(8,128)S(1)}, u32[]{:S(2)}, u32[]{:S(2)}) collective-permute-start(f32[1,4,2,128,128]{4,3,2,1,0:T(8,128)} %get-tuple-element.18), channel_id=1, source_target_pairs={{0,3},{1,2},{2,1},{3,0},{4,7},{5,6},{6,5},{7,4},{8,11},{9,10},{10,... | collective-permute-start | bytes 1572872 | tf_op jit(solution)/shard_map/ppermute | solution.py:350
  256.9 1.2 copy-start.1
  258.1 1.2 copy-start.2
